TPU v7x, 512 devices: a whole 4x8x8 slice. The times are simulated.
512 devices in a mesh: gz: 64 (over y, x, core), gy: 8 (over z).
Axes of the slice: x: 4, y: 8, z: 8, core: 2. Of those that a mesh axis runs over, the one named last changes fastest.
Arguments:
- fields: float32 [2, 512, 256, 512], P(None, 'gz', 'gy'), may hold values from 0 to 1
- classes: int32 [512, 256, 512], P('gz', 'gy'), may hold values from 0 to 7
- diff_table: float32 [2, 8], replicated, may hold values from 0.03 to 0.15
- transfer: float32 [4, 16], replicated, may hold values from 0.25 to 2
- bin_table: int32 [8], replicated, may hold values from 0 to 15
Outputs:
- species_out: float32 [2, 512, 256, 512], P(None, 'gz', 'gy')
- image: float32 [4, 131072], P(None, ('gy', 'gz'))
All inputs are finite; a program needn't handle non-finite values.
Results may differ from a plain program's by a relative error of at most 0.0003.
Values sent between devices are 32-bit elements; how exact they have to be, the bound alone decides.
A program may use at most 64 MiB of HBM per device.

v0:
```python
import jax
import jax.numpy as jnp
from jax import lax
from jax.sharding import Mesh
from jax.sharding import PartitionSpec as P

GZ = ("gz_0", "gz_1", "gz_2")
GY_GZ = ("gy", "gz_0", "gz_1", "gz_2")


FEED_RATE = 0.04
KILL_RATE = 0.06


def padded_2(shard, sides, width):
    edges = {}
    for axis, dim in sides:
        size, length = (lax.axis_size(axis), shard.shape[dim])
        up = [(i, (i + 1) % size) for i in range(size - 1)]
        last = lax.slice_in_dim(shard, length - width, length, axis=dim)
        first = lax.slice_in_dim(shard, 0, width, axis=dim)
        edges[dim] = (
            lax.ppermute(last, axis, up),
            lax.ppermute(first, axis, [(b, a) for a, b in up]),
        )
    done = []
    for _, dim in sides:
        low, high = edges[dim]
        around = [(width, width) if d in done else (0, 0) for d in range(shard.ndim)]
        shard = jnp.concatenate([jnp.pad(low, around), shard, jnp.pad(high, around)], axis=dim)
        done.append(dim)
    return shard


def extended(shard, sides, width):
    for axis, dim in sides:
        size, length = (lax.axis_size(axis), shard.shape[dim])
        up = [(i, (i + 1) % size) for i in range(size - 1)]
        down = [(j, i) for i, j in up]
        last = lax.slice_in_dim(shard, length - width, length, axis=dim)
        first = lax.slice_in_dim(shard, 0, width, axis=dim)
        before = lax.ppermute(last, axis, up)
        after = lax.ppermute(first, axis, down)
        shard = jnp.concatenate([before, shard, after], axis=dim)
    return shard


def in_blocks(shard, dim, length):
    lengths = shard.shape
    pieces = shard.reshape(*lengths[:dim], length, lengths[dim] // length, *lengths[dim + 1 :])
    return jnp.moveaxis(pieces, dim, 0)


def in_order(pieces, dim):
    lengths = list(pieces.shape[1:])
    lengths[dim] *= pieces.shape[0]
    return jnp.moveaxis(pieces, 0, dim).reshape(lengths)


def exchange_in_order(pieces, axes, sequence):
    inside = pieces.shape[1:]
    filled = pieces.reshape(*(lax.axis_size(a) for a in axes), *inside)
    for k in sequence:
        filled = lax.all_to_all(filled, axes[k], k, k, tiled=True)
    return filled.reshape(-1, *inside)


def exchange_by_chip(shard, groups, sequence, split_dim, concat_dim):
    length = lax.axis_size(groups[0]) * lax.axis_size(groups[1])
    pieces = in_blocks(shard, split_dim, length)
    return in_order(exchange_in_order(pieces, groups, sequence), concat_dim)


def per_class(classes, class_table):
    result = jnp.zeros((class_table.shape[0],) + classes.shape, jnp.float32)
    for material in range(class_table.shape[1]):
        column = class_table[:, material].reshape((-1,) + (1,) * classes.ndim)
        result = jnp.where((classes == material)[None], column, result)
    return result


def advance(padded, centre, cell_rates):
    widened = jnp.pad(padded, ((0, 0), (0, 0), (0, 0), (1, 1)))
    neighbours = widened[:, 2:, 1:-1, 1:-1] + widened[:, :-2, 1:-1, 1:-1]
    neighbours = neighbours + widened[:, 1:-1, 2:, 1:-1] + widened[:, 1:-1, :-2, 1:-1]
    neighbours = neighbours + widened[:, 1:-1, 1:-1, 2:] + widened[:, 1:-1, 1:-1, :-2]
    spread = cell_rates * (neighbours - 6.0 * centre)
    activator = centre[0]
    inhibitor = centre[1]
    growth = activator * inhibitor * inhibitor
    new_first = activator + spread[0] - growth + FEED_RATE * (1.0 - activator)
    new_second = inhibitor + spread[1] + growth - (FEED_RATE + KILL_RATE) * inhibitor
    return jnp.stack([new_first, new_second])


def render(fields, classes, colours, depth_step):

    def absorb(state_pair, planes):
        colour, transmit = state_pair
        activator, inhibitor, material = planes
        lookup = per_class(material, colours)
        extinction = lookup[3] * (0.25 + inhibitor * inhibitor)
        opacity = 1.0 - jnp.exp(-extinction * depth_step)
        colour = colour + (transmit * opacity * activator)[None] * lookup[:3]
        transmit = transmit * (1.0 - opacity)
        return ((colour, transmit), None)

    plane_shape = classes.shape[1:]
    initial = (jnp.zeros((3,) + plane_shape, jnp.float32), jnp.ones(plane_shape, jnp.float32))
    final_pair, unused = lax.scan(absorb, initial, (fields[0], fields[1], classes))
    return final_pair


def shards(fields, classes, diff_table, transfer, bin_table):
    depth_cells = classes.shape[0]
    rows_cells = classes.shape[1]
    slab_count = lax.axis_size(GZ)
    band_count = lax.axis_size("gy")
    depth_step = 2.0 / (depth_cells * slab_count)
    cell_rates = per_class(classes, diff_table)
    depth_index = (
        lax.axis_index(GZ) * depth_cells - 1 + jnp.arange(depth_cells + 2, dtype=jnp.int32)
    )
    row_index = lax.axis_index("gy") * rows_cells - 1 + jnp.arange(rows_cells + 2, dtype=jnp.int32)
    depth_inside = (depth_index >= 0) & (depth_index < depth_cells * slab_count)
    row_inside = (row_index >= 0) & (row_index < rows_cells * band_count)
    inside = depth_inside[:, None] & row_inside[None, :]
    rim_classes = padded_2(classes, ((GZ, 0), ("gy", 1)), 1)
    rim_rates = per_class(rim_classes, diff_table)
    padded = extended(fields, ((GZ, 1), ("gy", 2)), 2)
    middle = advance(padded, padded[:, 1:-1, 1:-1], rim_rates)
    middle = jnp.where(inside[None, :, :, None], middle, 0.0)
    fields = advance(middle, middle[:, 1:-1, 1:-1], cell_rates)
    chooser = (
        jnp.arange(transfer.shape[1], dtype=jnp.int32)[:, None] == bin_table[None, :]
    ).astype(jnp.float32)
    colours = jnp.dot(transfer, chooser, precision=lax.Precision.HIGHEST)
    colour, transmit = render(fields, classes, colours, depth_step)
    pixels = rows_cells * classes.shape[2]
    colour = colour.reshape(3, pixels)
    transmit = transmit.reshape(pixels)
    stacked = jnp.concatenate([colour, transmit[None]], 0).reshape(4, 1, pixels)
    received = exchange_by_chip(stacked, (("gz_0", "gz_1"), "gz_2"), (1, 0), 2, 1)
    slab_light = received[3]
    shifted = jnp.concatenate([jnp.ones_like(slab_light[:1]), slab_light[:-1]], 0)
    before = jnp.cumprod(shifted, axis=0)
    colour_sum = jnp.sum(received[:3] * before[None], axis=1)
    opacity_sum = jnp.sum(before * (1.0 - slab_light), axis=0)
    image = jnp.concatenate([colour_sum, opacity_sum[None]], 0)
    return (fields, image)


def solution(mesh):
    finer = Mesh(mesh.devices.reshape(8, 4, 2, mesh.shape["gy"]), ("gz_0", "gz_1", "gz_2", "gy"))
    return jax.shard_map(
        shards,
        mesh=finer,
        in_specs=(P(None, GZ, "gy", None), P(GZ, "gy", None), P(), P(), P()),
        out_specs=(P(None, GZ, "gy", None), P(None, GY_GZ)),
        check_vma=False,
    )
```

profile of v0, /device:TPU:192, one launch (start us, length us, event | category | flops | bytes accessed | tf_op | source)
XLA Modules:
  0.0 103.4 jit_solution(12304637047826986396)
XLA Ops:
  0.7 1.1 %fusion.32 = (f32[2,2,32,512]{3,2,1,0:T(8,128)S(1)}, f32[2,2,32,512]{3,2,1,0:T(8,128)S(1)}) fusion(f32[2,8,32,512]{3,2,1,0:T(8,128)} %param.7), kind=kLoop, calls=%fused_computation.118 | loop fusion | bytes 1048576 | tf_op jit(solution)/shard_map/slice | solution.py:41
  1.8 1.8 %collective-permute-start = (f32[2,2,32,512]{3,2,1,0:T(8,128)S(1)}, f32[2,2,32,512]{3,2,1,0:T(8,128)S(1)}, u32[]{:S(2)}, u32[]{:S(2)}) collective-permute-start(f32[2,2,32,512]{3,2,1,0:T(8,128)S(1)} %get-tuple-element.136), channel_id=1, source_target_pairs={{0,8},{8,16},{16,24},{24,32},{32,40},{40,48},{48,56},{56,64},{64,7... | collective-permute-start | bytes 786440 | tf_op jit(solution)/shard_map/ppermute | solution.py:42
  3.6 0.9 fusion.34
  4.5 3.7 %collective-permute-start.5 = (s32[1,32,512]{2,1,0:T(8,128)S(1)}, s32[1,32,512]{2,1,0:T(8,128)S(1)}, u32[]{:S(2)}, u32[]{:S(2)}) collective-permute-start(s32[1,32,512]{2,1,0:T(8,128)S(1)} %get-tuple-element.155), channel_id=1, source_target_pairs={{0,8},{8,16},{16,24},{24,32},{32,40},{40,48},{48,56},{56,64},{64,7... | collective-permute-start | bytes 196616 | tf_op jit(solution)/shard_map/ppermute | solution.py:23
  8.1 1.3 %collective-permute-start.6 = (s32[1,32,512]{2,1,0:T(8,128)S(1)}, s32[1,32,512]{2,1,0:T(8,128)S(1)}, u32[]{:S(2)}, u32[]{:S(2)}) collective-permute-start(s32[1,32,512]{2,1,0:T(8,128)S(1)} %get-tuple-element.156), channel_id=1, source_target_pairs={{8,0},{16,8},{24,16},{32,24},{40,32},{48,40},{56,48},{64,56},{72,6... | collective-permute-start | bytes 196616 | tf_op jit(solution)/shard_map/ppermute | solution.py:24
  9.4 1.0 fusion.33
  10.4 5.5 %collective-permute-start.4 = (s32[8,1,512]{2,1,0:T(1,128)S(1)}, s32[8,1,512]{2,1,0:T(1,128)S(1)}, u32[]{:S(2)}, u32[]{:S(2)}) collective-permute-start(s32[8,1,512]{2,1,0:T(1,128)S(1)} %get-tuple-element.153), channel_id=1, source_target_pairs={{0,1},{1,2},{2,3},{3,4},{4,5},{5,6},{6,7},{8,9},{9,10},{10,11},{11... | collective-permute-start | bytes 49160 | tf_op jit(solution)/shard_map/ppermute | solution.py:23
  15.9 1.9 %collective-permute-start.7 = (s32[8,1,512]{2,1,0:T(1,128)S(1)}, s32[8,1,512]{2,1,0:T(1,128)S(1)}, u32[]{:S(2)}, u32[]{:S(2)}) collective-permute-start(s32[8,1,512]{2,1,0:T(1,128)S(1)} %get-tuple-element.154), channel_id=1, source_target_pairs={{1,0},{2,1},{3,2},{4,3},{5,4},{6,5},{7,6},{9,8},{10,9},{11,10},{12... | collective-permute-start | bytes 49160 | tf_op jit(solution)/shard_map/ppermute | solution.py:24
  17.9 1.4 %broadcast_compare_fusion.15 = (pred[8,32,512]{2,1,0:T(8,128)(4,1)S(1)}, pred[8,32,512]{2,1,0:T(8,128)(4,1)S(1)}, pred[8,32,512]{2,1,0:T(8,128)(4,1)}, pred[8,32...) fusion(s32[8,32,512]{2,1,0:T(8,128)S(1)} %copy-done.1), kind=kLoop, calls=%fused_computation.91 | loop fusion | flops 1048576 | bytes 1572864 | tf_op jit(solution)/shard_map/eq | solution.py:78
  19.6 0.3 slice_reduce_fusion.7
  20.0 1.3 %collective-permute-start.1 = (f32[2,2,32,512]{3,2,1,0:T(8,128)S(1)}, f32[2,2,32,512]{3,2,1,0:T(8,128)S(1)}, u32[]{:S(2)}, u32[]{:S(2)}) collective-permute-start(f32[2,2,32,512]{3,2,1,0:T(8,128)S(1)} %get-tuple-element.135), channel_id=1, source_target_pairs={{8,0},{16,8},{24,16},{32,24},{40,32},{48,40},{56,48},{64,56},{72,6... | collective-permute-start | bytes 786440 | tf_op jit(solution)/shard_map/ppermute | solution.py:43
  21.3 1.5 %collective-permute-done.7 = s32[8,1,512]{2,1,0:T(1,128)S(1)} collective-permute-done((s32[8,1,512]{2,1,0:T(1,128)S(1)}, s32[8,1,512]{2,1,0:T(1,128)S(1)}, u32[]{:S(2)}, u32[]{:S(2)}) %collective-permute-start.7) | collective-permute-done | bytes 16416 | tf_op jit(solution)/shard_map/ppermute | solution.py:24
  22.8 0.4 broadcast_compare_fusion.7
  23.3 0.4 broadcast_compare_fusion.4
  23.9 4.8 %collective-permute-start.2 = (f32[2,12,2,512]{3,2,1,0:T(2,128)S(1)}, f32[2,12,2,512]{3,2,1,0:T(2,128)S(1)}, u32[]{:S(2)}, u32[]{:S(2)}) collective-permute-start(f32[2,12,2,512]{3,2,1,0:T(2,128)S(1)} %get-tuple-element.133), channel_id=1, source_target_pairs={{0,1},{1,2},{2,3},{3,4},{4,5},{5,6},{6,7},{8,9},{9,10},{10,11},{11... | collective-permute-start | bytes 294920 | tf_op jit(solution)/shard_map/ppermute | solution.py:42
  28.8 1.9 %collective-permute-start.3 = (f32[2,12,2,512]{3,2,1,0:T(2,128)S(1)}, f32[2,12,2,512]{3,2,1,0:T(2,128)S(1)}, u32[]{:S(2)}, u32[]{:S(2)}) collective-permute-start(f32[2,12,2,512]{3,2,1,0:T(2,128)S(1)} %get-tuple-element.134), channel_id=1, source_target_pairs={{1,0},{2,1},{3,2},{4,3},{5,4},{6,5},{7,6},{9,8},{10,9},{11,10},{12... | collective-permute-start | bytes 294920 | tf_op jit(solution)/shard_map/ppermute | solution.py:43
  30.7 0.3 broadcast_compare_fusion.1
  31.0 5.5 %collective-permute-done.3 = f32[2,12,2,512]{3,2,1,0:T(2,128)S(1)} collective-permute-done((f32[2,12,2,512]{3,2,1,0:T(2,128)S(1)}, f32[2,12,2,512]{3,2,1,0:T(2,128)S(1)}, u32[]{:S(2)}, u32[]{:S(2)}) %collective-permute-start.3) | collective-permute-done | bytes 98336 | tf_op jit(solution)/shard_map/ppermute | solution.py:43
  36.5 0.4 pad_maximum_fusion
  36.9 3.3 %fusion.9 = f32[2,10,34,512]{3,2,1,0:T(8,128)S(1)} fusion(f32[2,12,36,512]{3,2,1,0:T(8,128)S(1)} %pad_maximum_fusion, f32[2,12,32,512]{3,2,1,0:T(8,128)S(1)} %constant_dynamic-update-slice_fusion, f32[2,12,2,512]{3,2,1,0:T(2,128)S(1)} %collective-permute-done.2, f32[2,12,2,512]{3,2,1,0:T(2,128)S(1)} %collective-permute-done.3, f32[2]{0:T(128)S(1)} %get-tuple-element.93, ...), kind=kLoop, calls=%fused_computation.35 | loop fusion | flops 6266880 | bytes 11685888 | tf_op jit(solution)/shard_map/mul | solution.py:87
  40.2 0.4 fusion.19
  40.9 0.6 copy-done.3
  41.9 1.8 %fusion.15 = f32[2,8,32,512]{3,2,1,0:T(8,128)S(1)} fusion(f32[2,10,34,512]{3,2,1,0:T(8,128)S(1)} %maximum_select_fusion, f32[2]{0:T(128)S(1)} %copy-done.19, f32[2]{0:T(128)S(1)} %copy-done.21, f32[2]{0:T(128)S(1)} %get-tuple-element.88, f32[2]{0:T(128)S(1)} %copy-done.11, f32[2]{0:T(128)S(1)} %copy-done.13, f32[2]{0:T(128)S(1)} %copy-done.15, ...), kind=kLoop, calls=%fused_computation.48 | loop fusion | flops 4194304 | bytes 8982528 | tf_op jit(solution)/shard_map/mul | solution.py:87
  43.7 1.3 %fusion.21 = (f32[8,32,512]{2,1,0:T(8,128)}, f32[8,32,512]{2,1,0:T(8,128)}) fusion(f32[2,8,32,512]{3,2,1,0:T(8,128)S(1)} %fusion.15, f32[2,10,34,512]{3,2,1,0:T(8,128)S(1)} %maximum_select_fusion), kind=kLoop, calls=%fused_computation.66 | loop fusion | flops 1441792 | bytes 3145728 | tf_op jit(solution)/shard_map/add | solution.py:91
  45.0 22.9 %while.13 = (s32[]{:T(128)}, f32[3,32,512]{2,1,0:T(8,128)}, f32[32,512]{1,0:T(8,128)S(1)}, s32[8,32,512]{2,1,0:T(8,128)S(1)}, f32[4,8]{0,1:T(8,128)S(1)}, /*inde...) while((s32[]{:T(128)}, f32[3,32,512]{2,1,0:T(8,128)}, ...), condition=%wide.region_1.2_spmd.clone, body=%wide.region_0.1_spmd.clone.sunk | while | flops 983043 | bytes 1638896 | solution.py:110
  45.4 0.9 subtract_multiply_fusion.2
  46.4 0.7 fusion.37
  47.5 0.9 subtract_multiply_fusion.2
  48.4 1.7 %fusion.37 = f32[3,32,512]{2,1,0:T(8,128)} fusion(f32[4,32,512]{2,1,0:T(8,128)S(1)} %select_select_fusion.2, f32[3,32,512]{2,1,0:T(8,128)} %get-tuple-element.246, f32[32,512]{1,0:T(8,128)S(1)} %get-tuple-element.234, pred[]{:T(512)S(6)} %compare.7), kind=kLoop, calls=%fused_computation.2.clone.1 | loop fusion | flops 147456 | bytes 655361 | tf_op jit(solution)/shard_map/while/body/eval_jaxpr/add | solution.py:104
  50.5 0.9 subtract_multiply_fusion.2
  51.4 1.7 %fusion.37 = f32[3,32,512]{2,1,0:T(8,128)} fusion(f32[4,32,512]{2,1,0:T(8,128)S(1)} %select_select_fusion.2, f32[3,32,512]{2,1,0:T(8,128)} %get-tuple-element.246, f32[32,512]{1,0:T(8,128)S(1)} %get-tuple-element.234, pred[]{:T(512)S(6)} %compare.7), kind=kLoop, calls=%fused_computation.2.clone.1 | loop fusion | flops 147456 | bytes 655361 | tf_op jit(solution)/shard_map/while/body/eval_jaxpr/add | solution.py:104
  53.5 0.9 subtract_multiply_fusion.2
  54.4 1.7 %fusion.37 = f32[3,32,512]{2,1,0:T(8,128)} fusion(f32[4,32,512]{2,1,0:T(8,128)S(1)} %select_select_fusion.2, f32[3,32,512]{2,1,0:T(8,128)} %get-tuple-element.246, f32[32,512]{1,0:T(8,128)S(1)} %get-tuple-element.234, pred[]{:T(512)S(6)} %compare.7), kind=kLoop, calls=%fused_computation.2.clone.1 | loop fusion | flops 147456 | bytes 655361 | tf_op jit(solution)/shard_map/while/body/eval_jaxpr/add | solution.py:104
  56.4 0.9 subtract_multiply_fusion.2
  57.4 1.7 %fusion.37 = f32[3,32,512]{2,1,0:T(8,128)} fusion(f32[4,32,512]{2,1,0:T(8,128)S(1)} %select_select_fusion.2, f32[3,32,512]{2,1,0:T(8,128)} %get-tuple-element.246, f32[32,512]{1,0:T(8,128)S(1)} %get-tuple-element.234, pred[]{:T(512)S(6)} %compare.7), kind=kLoop, calls=%fused_computation.2.clone.1 | loop fusion | flops 147456 | bytes 655361 | tf_op jit(solution)/shard_map/while/body/eval_jaxpr/add | solution.py:104
  59.4 0.9 subtract_multiply_fusion.2
  60.3 1.7 %fusion.37 = f32[3,32,512]{2,1,0:T(8,128)} fusion(f32[4,32,512]{2,1,0:T(8,128)S(1)} %select_select_fusion.2, f32[3,32,512]{2,1,0:T(8,128)} %get-tuple-element.246, f32[32,512]{1,0:T(8,128)S(1)} %get-tuple-element.234, pred[]{:T(512)S(6)} %compare.7), kind=kLoop, calls=%fused_computation.2.clone.1 | loop fusion | flops 147456 | bytes 655361 | tf_op jit(solution)/shard_map/while/body/eval_jaxpr/add | solution.py:104
  62.4 0.9 subtract_multiply_fusion.2
  63.3 1.7 %fusion.37 = f32[3,32,512]{2,1,0:T(8,128)} fusion(f32[4,32,512]{2,1,0:T(8,128)S(1)} %select_select_fusion.2, f32[3,32,512]{2,1,0:T(8,128)} %get-tuple-element.246, f32[32,512]{1,0:T(8,128)S(1)} %get-tuple-element.234, pred[]{:T(512)S(6)} %compare.7), kind=kLoop, calls=%fused_computation.2.clone.1 | loop fusion | flops 147456 | bytes 655361 | tf_op jit(solution)/shard_map/while/body/eval_jaxpr/add | solution.py:104
  65.4 0.9 subtract_multiply_fusion.2
  66.3 1.7 %fusion.37 = f32[3,32,512]{2,1,0:T(8,128)} fusion(f32[4,32,512]{2,1,0:T(8,128)S(1)} %select_select_fusion.2, f32[3,32,512]{2,1,0:T(8,128)} %get-tuple-element.246, f32[32,512]{1,0:T(8,128)S(1)} %get-tuple-element.234, pred[]{:T(512)S(6)} %compare.7), kind=kLoop, calls=%fused_computation.2.clone.1 | loop fusion | flops 147456 | bytes 655361 | tf_op jit(solution)/shard_map/while/body/eval_jaxpr/add | solution.py:104
  68.0 1.0 concatenate.68
  69.4 6.8 %all_to_all.10 = f32[32,2,4,1,256]{4,0,2,3,1:T(8,128)S(1)} all-to-all(f32[32,2,4,1,256]{4,0,2,3,1:T(8,128)S(1)} %copy.16), channel_id=1, replica_groups=mesh['gz_0'=8,'gz_1'=4,'gz_2'=2,'gy'=8] {'gz_2'}, dimensions={1} | all-to-all | bytes 524288 | tf_op jit(solution)/shard_map/all_to_all | solution.py:64
  76.2 0.9 copy.17
  77.1 12.0 %all-to-all-start.1 = ((f32[32,2,4,1,256]{4,1,2,3,0:T(2,128)}), f32[32,2,4,1,256]{4,1,2,3,0:T(2,128)S(1)}, u32[]{:S(2)}, u32[]{:S(2)}) async-start(f32[32,2,4,1,256]{4,1,2,3,0:T(2,128)} %copy.17), calls=%async_computation.1 | async-start | bytes 524288 | tf_op jit(solution)/shard_map/all_to_all | solution.py:64
  89.4 1.1 %pad_maximum_fusion.3 = f32[2,8,32,512]{3,2,1,0:T(8,128)} fusion(f32[1,8,32,512]{3,2,1,0:T(8,128)S(1)} %get-tuple-element.132, f32[1,8,32,512]{3,2,1,0:T(8,128)S(1)} %get-tuple-element.131), kind=kLoop, calls=%fused_computation.53 | loop fusion | flops 262144 | bytes 2097152 | tf_op jit(solution)/shard_map/stack | solution.py:93
  90.5 11.9 %all-to-all-done.1 = f32[32,2,4,1,256]{4,1,2,3,0:T(2,128)S(1)} async-done(((f32[32,2,4,1,256]{4,1,2,3,0:T(2,128)}), f32[32,2,4,1,256]{4,1,2,3,0:T(2,128)S(1)}, u32[]{:S(2)}, u32[]{:S(2)}) %all-to-all-start.1) | async-done | bytes 262176 | tf_op jit(solution)/shard_map/all_to_all | solution.py:64
  102.8 0.6 pad_maximum_fusion.5
  (98 shorter events, 5.3 us)
Async XLA Ops:
  0.6 18.8 %copy-start = (f32[4,16]{1,0:T(4,128)S(1)}, f32[4,16]{1,0:T(4,128)}, u32[]{:S(2)}) copy-start(f32[4,16]{1,0:T(4,128)} %param.10) | copy-start | bytes 772
  0.6 17.2 %copy-start.1 = (s32[8,32,512]{2,1,0:T(8,128)S(1)}, s32[8,32,512]{2,1,0:T(8,128)}, u32[]{:S(2)}) copy-start(s32[8,32,512]{2,1,0:T(8,128)} %param.8) | copy-start | bytes 1572868
  0.7 18.8 %copy-start.22 = (s32[8]{0:T(128)S(1)}, s32[8]{0:T(128)}, u32[]{:S(2)}) copy-start(s32[8]{0:T(128)} %param.11) | copy-start | bytes 100
  0.7 18.9 %copy-start.9 = (f32[2,8]{1,0:T(2,128)S(1)}, f32[2,8]{1,0:T(2,128)}, u32[]{:S(2)}) copy-start(f32[2,8]{1,0:T(2,128)} %param.9) | copy-start | bytes 196
  1.8 21.8 %collective-permute-start = (f32[2,2,32,512]{3,2,1,0:T(8,128)S(1)}, f32[2,2,32,512]{3,2,1,0:T(8,128)S(1)}, u32[]{:S(2)}, u32[]{:S(2)}) collective-permute-start(f32[2,2,32,512]{3,2,1,0:T(8,128)S(1)} %get-tuple-element.136), channel_id=1, source_target_pairs={{0,8},{8,16},{16,24},{24,32},{32,40},{40,48},{48,56},{56,64},{64,7... | collective-permute-start | bytes 786440 | tf_op jit(solution)/shard_map/ppermute | solution.py:42
  4.5 18.4 %collective-permute-start.5 = (s32[1,32,512]{2,1,0:T(8,128)S(1)}, s32[1,32,512]{2,1,0:T(8,128)S(1)}, u32[]{:S(2)}, u32[]{:S(2)}) collective-permute-start(s32[1,32,512]{2,1,0:T(8,128)S(1)} %get-tuple-element.155), channel_id=1, source_target_pairs={{0,8},{8,16},{16,24},{24,32},{32,40},{40,48},{48,56},{56,64},{64,7... | collective-permute-start | bytes 196616 | tf_op jit(solution)/shard_map/ppermute | solution.py:23
  8.1 14.7 %collective-permute-start.6 = (s32[1,32,512]{2,1,0:T(8,128)S(1)}, s32[1,32,512]{2,1,0:T(8,128)S(1)}, u32[]{:S(2)}, u32[]{:S(2)}) collective-permute-start(s32[1,32,512]{2,1,0:T(8,128)S(1)} %get-tuple-element.156), channel_id=1, source_target_pairs={{8,0},{16,8},{24,16},{32,24},{40,32},{48,40},{56,48},{64,56},{72,6... | collective-permute-start | bytes 196616 | tf_op jit(solution)/shard_map/ppermute | solution.py:24
  10.4 9.6 %collective-permute-start.4 = (s32[8,1,512]{2,1,0:T(1,128)S(1)}, s32[8,1,512]{2,1,0:T(1,128)S(1)}, u32[]{:S(2)}, u32[]{:S(2)}) collective-permute-start(s32[8,1,512]{2,1,0:T(1,128)S(1)} %get-tuple-element.153), channel_id=1, source_target_pairs={{0,1},{1,2},{2,3},{3,4},{4,5},{5,6},{6,7},{8,9},{9,10},{10,11},{11... | collective-permute-start | bytes 49160 | tf_op jit(solution)/shard_map/ppermute | solution.py:23
  15.9 6.9 %collective-permute-start.7 = (s32[8,1,512]{2,1,0:T(1,128)S(1)}, s32[8,1,512]{2,1,0:T(1,128)S(1)}, u32[]{:S(2)}, u32[]{:S(2)}) collective-permute-start(s32[8,1,512]{2,1,0:T(1,128)S(1)} %get-tuple-element.154), channel_id=1, source_target_pairs={{1,0},{2,1},{3,2},{4,3},{5,4},{6,5},{7,6},{9,8},{10,9},{11,10},{12... | collective-permute-start | bytes 49160 | tf_op jit(solution)/shard_map/ppermute | solution.py:24
  19.3 4.4 %copy-start.2 = (f32[2,8,32,512]{3,2,1,0:T(8,128)S(1)}, f32[2,8,32,512]{3,2,1,0:T(8,128)}, u32[]{:S(2)}) copy-start(f32[2,8,32,512]{3,2,1,0:T(8,128)} %param.7) | copy-start | bytes 3145732
  19.9 17.0 %copy-start.10 = (f32[2]{0:T(128)}, f32[2]{0:T(128)S(1)}, u32[]{:S(2)}) copy-start(f32[2]{0:T(128)S(1)} %get-tuple-element.89) | copy-start | bytes 28
  19.9 17.0 %copy-start.12 = (f32[2]{0:T(128)}, f32[2]{0:T(128)S(1)}, u32[]{:S(2)}) copy-start(f32[2]{0:T(128)S(1)} %get-tuple-element.90) | copy-start | bytes 28
  19.9 17.0 %copy-start.14 = (f32[2]{0:T(128)}, f32[2]{0:T(128)S(1)}, u32[]{:S(2)}) copy-start(f32[2]{0:T(128)S(1)} %get-tuple-element.91) | copy-start | bytes 28
  19.9 17.0 %copy-start.16 = (f32[2]{0:T(128)}, f32[2]{0:T(128)S(1)}, u32[]{:S(2)}) copy-start(f32[2]{0:T(128)S(1)} %get-tuple-element.92) | copy-start | bytes 28
  19.9 17.0 %copy-start.18 = (f32[2]{0:T(128)}, f32[2]{0:T(128)S(1)}, u32[]{:S(2)}) copy-start(f32[2]{0:T(128)S(1)} %get-tuple-element.93) | copy-start | bytes 28
  19.9 17.0 %copy-start.20 = (f32[2]{0:T(128)}, f32[2]{0:T(128)S(1)}, u32[]{:S(2)}) copy-start(f32[2]{0:T(128)S(1)} %get-tuple-element.94) | copy-start | bytes 28
  20.0 3.8 %collective-permute-start.1 = (f32[2,2,32,512]{3,2,1,0:T(8,128)S(1)}, f32[2,2,32,512]{3,2,1,0:T(8,128)S(1)}, u32[]{:S(2)}, u32[]{:S(2)}) collective-permute-start(f32[2,2,32,512]{3,2,1,0:T(8,128)S(1)} %get-tuple-element.135), channel_id=1, source_target_pairs={{8,0},{16,8},{24,16},{32,24},{40,32},{48,40},{56,48},{64,56},{72,6... | collective-permute-start | bytes 786440 | tf_op jit(solution)/shard_map/ppermute | solution.py:43
  23.9 7.1 %collective-permute-start.2 = (f32[2,12,2,512]{3,2,1,0:T(2,128)S(1)}, f32[2,12,2,512]{3,2,1,0:T(2,128)S(1)}, u32[]{:S(2)}, u32[]{:S(2)}) collective-permute-start(f32[2,12,2,512]{3,2,1,0:T(2,128)S(1)} %get-tuple-element.133), channel_id=1, source_target_pairs={{0,1},{1,2},{2,3},{3,4},{4,5},{5,6},{6,7},{8,9},{9,10},{10,11},{11... | collective-permute-start | bytes 294920 | tf_op jit(solution)/shard_map/ppermute | solution.py:42
  28.8 7.7 %collective-permute-start.3 = (f32[2,12,2,512]{3,2,1,0:T(2,128)S(1)}, f32[2,12,2,512]{3,2,1,0:T(2,128)S(1)}, u32[]{:S(2)}, u32[]{:S(2)}) collective-permute-start(f32[2,12,2,512]{3,2,1,0:T(2,128)S(1)} %get-tuple-element.134), channel_id=1, source_target_pairs={{1,0},{2,1},{3,2},{4,3},{5,4},{6,5},{7,6},{9,8},{10,9},{11,10},{12... | collective-permute-start | bytes 294920 | tf_op jit(solution)/shard_map/ppermute | solution.py:43
  40.6 0.9 copy-start.3
  40.7 1.0 copy-start.4
  40.7 1.0 copy-start.5
  40.7 1.1 %copy-start.6 = (pred[8,32,512]{2,1,0:T(8,128)(4,1)S(1)}, pred[8,32,512]{2,1,0:T(8,128)(4,1)}, u32[]{:S(2)}) copy-start(pred[8,32,512]{2,1,0:T(8,128)(4,1)} %get-tuple-element.150) | copy-start | bytes 393220
  40.7 1.1 %copy-start.7 = (pred[8,32,512]{2,1,0:T(8,128)(4,1)S(1)}, pred[8,32,512]{2,1,0:T(8,128)(4,1)}, u32[]{:S(2)}) copy-start(pred[8,32,512]{2,1,0:T(8,128)(4,1)} %get-tuple-element.151) | copy-start | bytes 393220
  40.7 1.2 %copy-start.8 = (pred[8,32,512]{2,1,0:T(8,128)(4,1)S(1)}, pred[8,32,512]{2,1,0:T(8,128)(4,1)}, u32[]{:S(2)}) copy-start(pred[8,32,512]{2,1,0:T(8,128)(4,1)} %get-tuple-element.152) | copy-start | bytes 393220
  40.7 1.2 %copy-start.11 = (f32[2]{0:T(128)S(1)}, f32[2]{0:T(128)}, u32[]{:S(2)}) copy-start(f32[2]{0:T(128)} %copy-done.10) | copy-start | bytes 28
  40.7 1.1 %copy-start.13 = (f32[2]{0:T(128)S(1)}, f32[2]{0:T(128)}, u32[]{:S(2)}) copy-start(f32[2]{0:T(128)} %copy-done.12) | copy-start | bytes 28
  40.7 1.1 %copy-start.15 = (f32[2]{0:T(128)S(1)}, f32[2]{0:T(128)}, u32[]{:S(2)}) copy-start(f32[2]{0:T(128)} %copy-done.14) | copy-start | bytes 28
  40.7 1.1 %copy-start.17 = (f32[2]{0:T(128)S(1)}, f32[2]{0:T(128)}, u32[]{:S(2)}) copy-start(f32[2]{0:T(128)} %copy-done.16) | copy-start | bytes 28
  40.7 1.1 %copy-start.19 = (f32[2]{0:T(128)S(1)}, f32[2]{0:T(128)}, u32[]{:S(2)}) copy-start(f32[2]{0:T(128)} %copy-done.18) | copy-start | bytes 28
  40.8 1.1 %copy-start.21 = (f32[2]{0:T(128)S(1)}, f32[2]{0:T(128)}, u32[]{:S(2)}) copy-start(f32[2]{0:T(128)} %copy-done.20) | copy-start | bytes 28
  77.1 25.3 %all-to-all-start.1 = ((f32[32,2,4,1,256]{4,1,2,3,0:T(2,128)}), f32[32,2,4,1,256]{4,1,2,3,0:T(2,128)S(1)}, u32[]{:S(2)}, u32[]{:S(2)}) async-start(f32[32,2,4,1,256]{4,1,2,3,0:T(2,128)} %copy.17), calls=%async_computation.1 | async-start | bytes 524288 | tf_op jit(solution)/shard_map/all_to_all | solution.py:64
where the time goes:
time: 104 us; the launch traced here: 103 us
  other arithmetic  34.9 us (34%)
  starting transfers between devices  34.1 us (33%)
  waiting for transfers between devices  18.9 us (18%)
  local copies, waits for them, and re-layouts  7.07 us (7%)
  blocking collectives  6.85 us (7%)
  between operations  1.19 us (1%)
    add x8, other arithmetic, absorb(): colour = colour + (transmit * opacity * activator)[None] * lookup[:3]  12.3 us
    all_to_all x1, starting transfers between devices, exchange_in_order(): filled = lax.all_to_all(filled, axes[k], k, k, tiled=True)  12 us
    all_to_all x1, waiting for transfers between devices, exchange_in_order(): filled = lax.all_to_all(filled, axes[k], k, k, tiled=True)  11.9 us
    ppermute x2, starting transfers between devices, padded_2(): lax.ppermute(last, axis, up)  9.16 us
    mul x8, other arithmetic, absorb(): transmit = transmit * (1.0 - opacity)  7.39 us
    all_to_all x1, blocking collectives, exchange_in_order(): filled = lax.all_to_all(filled, axes[k], k, k, tiled=True)  6.85 us
    ppermute x2, starting transfers between devices, extended(): before = lax.ppermute(last, axis, up)  6.57 us
    ppermute x2, waiting for transfers between devices, extended(): after = lax.ppermute(first, axis, down)  5.48 us
  transfers between devices with their start and end apart: 9, of which 3 were waited for; matrix products, arithmetic and copies ran while one was open for 6% of the time, Pallas kernels for 0%

commit v1 on v0

v1 whole, which is shorter than its diff:
```python
import functools

import jax
import jax.numpy as jnp
from jax import lax
from jax.experimental import pallas as pl
from jax.experimental.pallas import tpu as pltpu
from jax.sharding import Mesh
from jax.sharding import PartitionSpec as P

MESH = pl.DeviceIdType.MESH
NAMES = ("py", "px", "pc", "pz")
GZ = ("py", "px", "pc")
FEED_RATE = 0.04
KILL_RATE = 0.06
NCLASS = 8
DEPTH = 8
COLS = 512
HALF = 256
BLOCK = 8


def kernel(
    sizes, depth_step,
    fields, classes, diff_table, transfer, bin_table,
    species, image,
    pad0, pad1, final, cls, rates, look, mid, part,
    edge0, edge0_in, edge1, edge1_in,
    send_a, recv_a, send_b, recv_b,
    diff_s, trans_s, bin_s,
    load_sem, table_sem, out_sem, own_sem,
    z_send, z_recv, y_send, y_recv, a_send, a_recv, b_send, b_recv,
):
    ny, nx, nc, nz = sizes
    py, px, pc, pz = (lax.axis_index(name) for name in NAMES)
    slabs = ny * nx * nc
    groups = (ny * nx) // BLOCK
    slab = (py * nx + px) * nc + pc

    def slab_device(g):
        return (lax.div(g, nx * nc), lax.rem(lax.div(g, nc), nx), lax.rem(g, nc), pz)

    above = slab_device(lax.rem(slab + 1, slabs))
    below = slab_device(lax.rem(slab + slabs - 1, slabs))
    north = (py, px, pc, lax.rem(pz + nz - 1, nz))
    south = (py, px, pc, lax.rem(pz + 1, nz))
    team = nx * nc
    me_a = px * nc + pc

    def mate_a(j):
        i = lax.rem(me_a + j, team)
        return i, (py, lax.div(i, nc), lax.rem(i, nc), pz)

    def mate_b(j):
        i = lax.rem(py + j, ny)
        return i, (i, px, pc, pz)

    load_fields = pltpu.make_async_copy(fields, pad0.at[:, pl.ds(1, DEPTH)], load_sem.at[0])
    load_classes = pltpu.make_async_copy(classes, cls, load_sem.at[1])
    load_fields.start()
    load_classes.start()
    tables = [
        pltpu.make_async_copy(src, dst, table_sem.at[i])
        for i, (src, dst) in enumerate(((diff_table, diff_s), (transfer, trans_s), (bin_table, bin_s)))
    ]
    for copy in tables:
        copy.start()
    barrier = pltpu.get_barrier_semaphore()
    partners = [above, below, north, south]
    partners += [mate_a(j)[1] for j in range(1, team)] + [mate_b(j)[1] for j in range(1, ny)]
    for device in partners:
        pl.semaphore_signal(barrier, inc=1, device_id=device, device_id_type=MESH)
    pl.semaphore_wait(barrier, len(partners))

    def depth_copies(step, source, first, last, target):
        made = []
        for k in range(groups):
            rows = pl.ds(BLOCK * k, BLOCK)
            for side, device, layer, place in ((0, above, last, 0), (1, below, first, DEPTH + 1)):
                made.append(
                    pltpu.make_async_remote_copy(
                        src_ref=source.at[:, layer, rows],
                        dst_ref=target.at[:, place, rows],
                        send_sem=z_send.at[step, side, k],
                        recv_sem=z_recv.at[step, side, k],
                        device_id=device,
                        device_id_type=MESH,
                    )
                )
        return made

    depth0 = depth_copies(0, fields, 0, DEPTH - 1, pad0)
    for copy in depth0:
        copy.start()
    load_fields.wait()

    def row_copies(step, part_at, source, target, layers):
        return [
            pltpu.make_async_remote_copy(
                src_ref=source.at[side, :, layers],
                dst_ref=target.at[side, :, layers],
                send_sem=y_send.at[step, part_at, side],
                recv_sem=y_recv.at[step, part_at, side],
                device_id=device,
                device_id_type=MESH,
            )
            for side, device in ((0, south), (1, north))
        ]

    def pack_rows(source, target, layers):
        for s in range(2):
            for z in layers:
                target[0, s, z] = source[s, z + 1, BLOCK * groups - 1 : BLOCK * groups, :]
                target[1, s, z] = source[s, z + 1, 0:1, :]

    pack_rows(pad0, edge0, range(DEPTH))
    rows0 = row_copies(0, 0, edge0, edge0_in, pl.ds(0, DEPTH))
    for copy in rows0:
        copy.start()

    for copy in tables:
        copy.wait()
    load_classes.wait()

    def class_bits(z, k):
        c = cls[z, BLOCK * k : BLOCK * k + BLOCK, :]
        return [(c & bit) != 0 for bit in (1, 2, 4)]

    def pick(bits, values):
        for bit in bits:
            values = [jnp.where(bit, high, low) for low, high in zip(values[::2], values[1::2])]
        return values[0]

    def look_up(target, values):
        splat = [[jnp.full((BLOCK, COLS), x, jnp.float32) for x in v] for v in values]

        def body(z, carry):
            for k in range(groups):
                bits = class_bits(z, k)
                for s, v in enumerate(splat):
                    target[s, z, BLOCK * k : BLOCK * k + BLOCK, :] = pick(bits, v)
            return carry

        lax.fori_loop(0, DEPTH, body, 0)

    look_up(rates, [[diff_s[s, m] for m in range(NCLASS)] for s in range(2)])

    sub = lax.broadcasted_iota(jnp.int32, (BLOCK, COLS), 0)
    col = lax.broadcasted_iota(jnp.int32, (BLOCK, COLS), 1)
    top, bottom = sub == 0, sub == BLOCK - 1
    left, right = col == 0, col == COLS - 1

    def around(source, edges, s, z, k):
        rows = slice(BLOCK * k, BLOCK * k + BLOCK)
        centre = source[s, z + 1, rows, :]
        if k == 0:
            before = edges[0, s, z]
        else:
            before = source[s, z + 1, BLOCK * k - 1 : BLOCK * k, :]
        if k == groups - 1:
            after = edges[1, s, z]
        else:
            after = source[s, z + 1, BLOCK * k + BLOCK : BLOCK * k + BLOCK + 1, :]
        total = source[s, z + 2, rows, :] + source[s, z, rows, :]
        total = total + jnp.where(bottom, after, pltpu.roll(centre, BLOCK - 1, 0))
        total = total + jnp.where(top, before, pltpu.roll(centre, 1, 0))
        total = total + jnp.where(right, 0.0, pltpu.roll(centre, COLS - 1, 1))
        total = total + jnp.where(left, 0.0, pltpu.roll(centre, 1, 1))
        return centre, total - 6.0 * centre

    def advance(source, edges, z, k):
        rows = slice(BLOCK * k, BLOCK * k + BLOCK)
        u, lap_u = around(source, edges, 0, z, k)
        v, lap_v = around(source, edges, 1, z, k)
        growth = u * v * v
        new_u = u + rates[0, z, rows, :] * lap_u - growth + FEED_RATE * (1.0 - u)
        new_v = v + rates[1, z, rows, :] * lap_v + growth - (FEED_RATE + KILL_RATE) * v
        return new_u, new_v

    def first_update(z, k):
        new_u, new_v = advance(pad0, edge0_in, z, k)
        rows = slice(BLOCK * k, BLOCK * k + BLOCK)
        pad1[0, z + 1, rows, :] = new_u
        pad1[1, z + 1, rows, :] = new_v

    def clear_rows(target, layers):
        @pl.when(pz == 0)
        def _():
            for s in range(2):
                for z in layers:
                    target[0, s, z] = jnp.zeros((1, COLS), jnp.float32)

        @pl.when(pz == nz - 1)
        def _():
            for s in range(2):
                for z in layers:
                    target[1, s, z] = jnp.zeros((1, COLS), jnp.float32)

    def clear_depth(target, side, k):
        rows = slice(BLOCK * k, BLOCK * k + BLOCK)

        @pl.when(slab == (0 if side == 0 else slabs - 1))
        def _():
            for s in range(2):
                target[s, 0 if side == 0 else DEPTH + 1, rows, :] = jnp.zeros((BLOCK, COLS), jnp.float32)

    for copy in rows0:
        copy.wait_recv()
    clear_rows(edge0_in, range(DEPTH))

    def interior1(z, carry):
        for k in range(groups):
            first_update(z, k)
        return carry

    lax.fori_loop(1, DEPTH - 1, interior1, 0)
    pack_rows(pad1, edge1, range(1, DEPTH - 1))
    rows1 = row_copies(1, 0, edge1, edge1_in, pl.ds(1, DEPTH - 2))
    for copy in rows1:
        copy.start()

    depth1 = depth_copies(1, pad1, 1, DEPTH, pad1)
    for k in range(groups):
        for side in range(2):
            depth0[2 * k + side].wait_recv()
            clear_depth(pad0, side, k)
            first_update(0 if side == 0 else DEPTH - 1, k)
            depth1[2 * k + 1 - side].start()
    pack_rows(pad1, edge1, (0, DEPTH - 1))
    rows2 = row_copies(1, 1, edge1, edge1_in, pl.ds(0, 1)) + row_copies(1, 2, edge1, edge1_in, pl.ds(DEPTH - 1, 1))
    for copy in rows2:
        copy.start()

    bins = [bin_s[m] for m in range(NCLASS)]
    look_up(look, [[trans_s[c, b] for b in bins] for c in range(4)])

    def second_update(z, k):
        new_u, new_v = advance(pad1, edge1_in, z, k)
        rows = slice(BLOCK * k, BLOCK * k + BLOCK)
        final[0, z, rows, :] = new_u
        final[1, z, rows, :] = new_v
        passed = jnp.exp(look[3, z, rows, :] * (0.25 + new_v * new_v) * (-depth_step))
        return new_u, passed

    for copy in rows1:
        copy.wait_recv()
    clear_rows(edge1_in, range(1, DEPTH - 1))
    for k in range(groups):
        rows = slice(BLOCK * k, BLOCK * k + BLOCK)
        mid[3, rows, :] = jnp.ones((BLOCK, COLS), jnp.float32)
        for c in range(3):
            mid[c, rows, :] = jnp.zeros((BLOCK, COLS), jnp.float32)

    def interior2(z, carry):
        for k in range(groups):
            rows = slice(BLOCK * k, BLOCK * k + BLOCK)
            new_u, passed = second_update(z, k)
            transmit = mid[3, rows, :]
            weight = transmit * (1.0 - passed) * new_u
            for c in range(3):
                mid[c, rows, :] = mid[c, rows, :] + weight * look[c, z, rows, :]
            mid[3, rows, :] = transmit * passed
        return carry

    lax.fori_loop(1, DEPTH - 1, interior2, 0)

    for copy in rows2:
        copy.wait_recv()
    clear_rows(edge1_in, (0, DEPTH - 1))
    for k in range(groups):
        rows = slice(BLOCK * k, BLOCK * k + BLOCK)
        for side in range(2):
            depth1[2 * k + side].wait_recv()
            clear_depth(pad1, side, k)
        front_u, front_t = second_update(0, k)
        back_u, back_t = second_update(DEPTH - 1, k)
        front = (1.0 - front_t) * front_u
        transmit = mid[3, rows, :]
        back = transmit * (1.0 - back_t) * back_u
        values = [
            front * look[c, 0, rows, :] + front_t * (mid[c, rows, :] + back * look[c, DEPTH - 1, rows, :])
            for c in range(3)
        ]
        values.append(front_t * transmit * back_t)
        for c in range(4):
            for t in range(COLS // 128):
                part[c, t, rows, :] = values[c][:, 128 * t : 128 * t + 128]

    store = pltpu.make_async_copy(final, species, out_sem.at[0])
    store.start()

    tiles = COLS // 128 // nc
    for x in range(nx):
        for c in range(4):
            for t in range(COLS // 128):
                send_a[x * nc + t // tiles, c, :, 128 * (t % tiles) : 128 * (t % tiles) + 128] = part[
                    c, t, pl.ds(x, ny, stride=nx), :
                ]
    own = pltpu.make_async_copy(send_a.at[me_a], recv_a.at[me_a], own_sem.at[0])
    own.start()
    stage_a = []
    for j in range(1, team):
        i, device = mate_a(j)
        copy = pltpu.make_async_remote_copy(
            src_ref=send_a.at[i],
            dst_ref=recv_a.at[me_a],
            send_sem=a_send.at[j],
            recv_sem=a_recv.at[me_a],
            device_id=device,
            device_id_type=MESH,
        )
        copy.start()
        stage_a.append(copy)
    own.wait()
    for j in range(1, team):
        i, device = mate_a(j)
        pltpu.make_async_remote_copy(
            src_ref=send_a.at[i],
            dst_ref=recv_a.at[i],
            send_sem=a_send.at[j],
            recv_sem=a_recv.at[i],
            device_id=device,
            device_id_type=MESH,
        ).wait_recv()
    for t in range(HALF // 128):
        cols = slice(128 * t, 128 * t + 128)
        colour = [recv_a[0, c, :, cols] for c in range(3)]
        transmit = recv_a[0, 3, :, cols]
        for i in range(1, team):
            colour = [colour[c] + transmit * recv_a[i, c, :, cols] for c in range(3)]
            transmit = transmit * recv_a[i, 3, :, cols]
        for c, value in enumerate(colour + [transmit]):
            send_b[pl.ds(4 * t + c, ny, stride=8), :] = value

    own_b = pltpu.make_async_copy(send_b.at[pl.ds(pl.multiple_of(8 * py, 8), 8)], recv_b.at[py], own_sem.at[1])
    own_b.start()
    stage_b = []
    for j in range(1, ny):
        i, device = mate_b(j)
        copy = pltpu.make_async_remote_copy(
            src_ref=send_b.at[pl.ds(pl.multiple_of(8 * i, 8), 8)],
            dst_ref=recv_b.at[py],
            send_sem=b_send.at[j],
            recv_sem=b_recv.at[py],
            device_id=device,
            device_id_type=MESH,
        )
        copy.start()
        stage_b.append(copy)
    own_b.wait()
    for j in range(1, ny):
        i, device = mate_b(j)
        pltpu.make_async_remote_copy(
            src_ref=send_b.at[pl.ds(pl.multiple_of(8 * i, 8), 8)],
            dst_ref=recv_b.at[i],
            send_sem=b_send.at[j],
            recv_sem=b_recv.at[i],
            device_id=device,
            device_id_type=MESH,
        ).wait_recv()
    lower = lax.broadcasted_iota(jnp.int32, (8, 128), 0) < 4
    total = recv_b[0]
    transmit = None
    for i in range(ny):
        value = recv_b[i]
        light = jnp.where(lower, recv_b[i, 3:4, :], recv_b[i, 7:8, :])
        if i == 0:
            total, transmit = value, light
        else:
            total, transmit = total + transmit * value, transmit * light
    place = lax.broadcasted_iota(jnp.int32, (8, 128), 0)
    total = jnp.where((place == 3) | (place == 7), 1.0 - transmit, total)
    image[:, 0:128] = total[0:4, :]
    image[:, 128:256] = total[4:8, :]

    for copy in depth0 + rows0 + rows1 + depth1 + rows2 + stage_a + stage_b:
        copy.wait_send()
    store.wait()


def build(mesh, sizes):
    ny, nx, nc, nz = sizes
    rows = ny * nx
    groups = rows // BLOCK
    team = nx * nc
    f32 = jnp.float32

    def shards(fields, classes, diff_table, transfer, bin_table):
        depth_step = 2.0 / (DEPTH * ny * nx * nc)
        anywhere = pl.BlockSpec(memory_space=pl.ANY)
        return pl.pallas_call(
            functools.partial(kernel, sizes, depth_step),
            out_shape=(
                jax.ShapeDtypeStruct((2, DEPTH, rows, COLS), f32),
                jax.ShapeDtypeStruct((4, HALF), f32),
            ),
            in_specs=[anywhere] * 5,
            out_specs=(anywhere, pl.BlockSpec(memory_space=pltpu.VMEM)),
            scratch_shapes=[
                pltpu.VMEM((2, DEPTH + 2, rows, COLS), f32),
                pltpu.VMEM((2, DEPTH + 2, rows, COLS), f32),
                pltpu.VMEM((2, DEPTH, rows, COLS), f32),
                pltpu.VMEM((DEPTH, rows, COLS), jnp.int32),
                pltpu.VMEM((2, DEPTH, rows, COLS), f32),
                pltpu.VMEM((4, DEPTH, rows, COLS), f32),
                pltpu.VMEM((4, rows, COLS), f32),
                pltpu.VMEM((4, COLS // 128, rows, 128), f32),
                pltpu.VMEM((2, 2, DEPTH, 1, COLS), f32),
                pltpu.VMEM((2, 2, DEPTH, 1, COLS), f32),
                pltpu.VMEM((2, 2, DEPTH, 1, COLS), f32),
                pltpu.VMEM((2, 2, DEPTH, 1, COLS), f32),
                pltpu.VMEM((team, 4, ny, HALF), f32),
                pltpu.VMEM((team, 4, ny, HALF), f32),
                pltpu.VMEM((8 * ny, 128), f32),
                pltpu.VMEM((ny, 8, 128), f32),
                pltpu.SMEM((2, NCLASS), f32),
                pltpu.SMEM(transfer.shape, f32),
                pltpu.SMEM(bin_table.shape, jnp.int32),
                pltpu.SemaphoreType.DMA((2,)),
                pltpu.SemaphoreType.DMA((3,)),
                pltpu.SemaphoreType.DMA((1,)),
                pltpu.SemaphoreType.DMA((2,)),
                pltpu.SemaphoreType.DMA((2, 2, groups)),
                pltpu.SemaphoreType.DMA((2, 2, groups)),
                pltpu.SemaphoreType.DMA((2, 3, 2)),
                pltpu.SemaphoreType.DMA((2, 3, 2)),
                pltpu.SemaphoreType.DMA((team,)),
                pltpu.SemaphoreType.DMA((team,)),
                pltpu.SemaphoreType.DMA((ny,)),
                pltpu.SemaphoreType.DMA((ny,)),
            ],
            compiler_params=pltpu.CompilerParams(
                collective_id=0, has_side_effects=True
            ),
            name="gray_scott",
        )(fields, classes, diff_table, transfer, bin_table)

    finer = Mesh(mesh.devices.reshape(sizes), NAMES)
    return jax.shard_map(
        shards,
        mesh=finer,
        in_specs=(P(None, GZ, "pz", None), P(GZ, "pz", None), P(), P(), P()),
        out_specs=(P(None, GZ, "pz", None), P(None, ("pz",) + GZ)),
        check_vma=False,
    )


def solution(mesh):
    return build(mesh, (8, 4, 2, mesh.shape["gy"]))
```

time: 104 us -> 38.5 us (0.37)
  the two profiles are of different devices: /device:TPU:192 before, /device:TPU:1 now
where the time goes in v1:
time: 38.5 us; the launch traced here: 38.4 us
  Pallas kernels  34.8 us (90%)
  local copies, waits for them, and re-layouts  2.89 us (8%)
  between operations  0.65 us (2%)
    pallas_call x1, Pallas kernels, shards(): pl.pallas_call(functools.partial(kernel, sizes, depth_step), out_shape=(j...  34.8 us
    unnamed x4, local copies, waits for them, and re-layouts  2.89 us

profile of v1, /device:TPU:1, one launch (start us, length us, event | category | flops | bytes accessed | tf_op | source)
XLA Modules:
  0.0 38.4 jit_solution(6819249459593008254)
XLA Ops:
  0.6 34.8 %gray_scott.1 = (f32[2,8,32,512]{3,2,1,0:T(8,128)}, f32[4,256]{1,0:T(4,128)}) custom-call(f32[2,8,32,512]{3,2,1,0:T(8,128)} %fields.1, s32[8,32,512]{2,1,0:T(8,128)} %classes.1, f32[2,8]{1,0:T(2,128)} %diff_table.1, f32[4,16]{1,0:T(4,128)} %transfer.1, s32[8]{0:T(128)} %bin_table.1), custom_call_target="tpu_custom_call" | custom-call | tf_op jit(solution)/shard_map/gray_scott/pallas_call | solution.py:391
  35.5 0.0 copy-start
  35.5 2.3 %copy.9 = f32[2,8,32,512]{3,2,1,0:T(8,128)} copy(f32[2,8,32,512]{3,2,1,0:T(8,128)} %get-tuple-element.4) | data formatting | bytes 2097152
  37.8 0.0 copy-done
  37.8 0.6 %copy.10 = f32[4,256]{1,0:T(4,128)} copy(f32[4,256]{1,0:T(4,128)S(1)} %copy-done) | data formatting | bytes 8192
Async XLA Ops:
  35.5 2.3 %copy-start = (f32[4,256]{1,0:T(4,128)S(1)}, f32[4,256]{1,0:T(4,128)}, u32[]{:S(2)}) copy-start(f32[4,256]{1,0:T(4,128)} %get-tuple-element.5) | copy-start | bytes 12292

commit v2 on v0

v2 whole, which is shorter than its diff:
```python
import functools

import jax
import jax.numpy as jnp
from jax import lax
from jax.experimental import pallas as pl
from jax.experimental.pallas import tpu as pltpu
from jax.sharding import Mesh
from jax.sharding import PartitionSpec as P

MESH = pl.DeviceIdType.MESH
NAMES = ("py", "px", "pc", "pz")
GZ = ("py", "px", "pc")
FEED_RATE = 0.04
KILL_RATE = 0.06
NCLASS = 8
DEPTH = 8
COLS = 512
LANES = 128
BLOCK = 8
F32 = jnp.float32


def span(k):
    return slice(BLOCK * k, BLOCK * k + BLOCK)


def kernel(
    sizes, depth_step,
    fields, classes, diff_table, transfer, bin_table,
    final, pixels,
    pad0, pad1, cls, rates, look, mid,
    edge0, edge0_in, edge1, edge1_in,
    halves, merged, gathered,
    diff_s, trans_s, bin_s,
    load_sem, class_sem, table_sem,
    z_send, z_recv, y_send, y_recv, c_send, c_recv, e_send, e_recv, relay,
):
    ny, nx, nc, nz = sizes
    py, px, pc, pz = (lax.axis_index(name) for name in NAMES)
    slabs = ny * nx * nc
    groups = (ny * nx) // BLOCK
    inner, outer = list(range(1, groups - 1)), [0, groups - 1]
    slab = (py * nx + px) * nc + pc
    chip = py * nx + px

    def slab_device(g):
        return (lax.div(g, nx * nc), lax.rem(lax.div(g, nc), nx), lax.rem(g, nc), pz)

    above = slab_device(lax.rem(slab + 1, slabs))
    below = slab_device(lax.rem(slab + slabs - 1, slabs))
    north = (py, px, pc, lax.rem(pz + nz - 1, nz))
    south = (py, px, pc, lax.rem(pz + 1, nz))
    mate = (py, px, 1 - pc, pz)
    has_above, has_below = slab < slabs - 1, slab > 0
    has_north, has_south = pz > 0, pz < nz - 1

    def shifted(dy, dx):
        return (lax.rem(py + dy, ny), lax.rem(px + dx, nx), pc, pz)

    loads = {
        k: pltpu.make_async_copy(
            fields.at[:, :, pl.ds(BLOCK * k, BLOCK)],
            pad0.at[:, pl.ds(1, DEPTH), pl.ds(BLOCK * k, BLOCK)],
            load_sem.at[k],
        )
        for k in outer + inner
    }
    for copy in loads.values():
        copy.start()
    tables = [
        pltpu.make_async_copy(src, dst, table_sem.at[i])
        for i, (src, dst) in enumerate(((diff_table, diff_s), (transfer, trans_s), (bin_table, bin_s)))
    ]
    for copy in tables:
        copy.start()
    load_classes = pltpu.make_async_copy(classes, cls, class_sem.at[0])
    load_classes.start()

    barrier = pltpu.get_barrier_semaphore()

    def greet(device):
        pl.semaphore_signal(barrier, inc=1, device_id=device, device_id_type=MESH)

    ring_y = (shifted(1, 0), shifted(ny - 1, 0))
    ring_x = (shifted(0, 1), shifted(0, nx - 1))
    partners = (mate,) + ring_x + ring_y
    others = ((has_above, above), (has_below, below), (has_north, north), (has_south, south))
    count = len(partners)
    for exists, device in others:
        pl.when(exists)(functools.partial(greet, device))
        count = count + jnp.where(exists, 1, 0)
    for device in partners:
        greet(device)
    pl.semaphore_wait(barrier, count)

    def pass_on(r, ring):
        for way in range(2):
            pl.semaphore_signal(relay.at[r, way], inc=1, device_id=ring[way], device_id_type=MESH)

    def heard(r):
        for way in range(2):
            pl.semaphore_wait(relay.at[r, way], 1)

    sends = {"up": has_above, "down": has_below, "south": has_south, "north": has_north}
    arrives = {"up": has_below, "down": has_above, "south": has_north, "north": has_south}

    def start(copies):
        for way, copy in copies:
            pl.when(sends[way])(copy.start)

    def arrive(copies, clear):
        for way, copy in copies:
            pl.when(arrives[way])(copy.wait_recv)
            pl.when(jnp.logical_not(arrives[way]))(functools.partial(clear, way))

    def depth_copy(step, way, k, source, target):
        side = ("up", "down").index(way)
        rows = pl.ds(BLOCK * k, BLOCK)
        return way, pltpu.make_async_remote_copy(
            src_ref=source[:, rows],
            dst_ref=target.at[:, (0, DEPTH + 1)[side], rows],
            send_sem=z_send.at[step, side, k],
            recv_sem=z_recv.at[step, side, k],
            device_id=(above, below)[side],
            device_id_type=MESH,
        )

    class Layer:
        def __init__(self, ref, z):
            self.ref, self.z = ref, z

        def __getitem__(self, at):
            return self.ref.at[at[0], self.z, at[1]]

    depth0 = {
        (way, k): depth_copy(0, way, k, Layer(fields, z), pad0)
        for k in inner + outer
        for way, z in (("up", DEPTH - 1), ("down", 0))
    }
    depth1 = {
        (way, k): depth_copy(1, way, k, Layer(pad1, z), pad1)
        for k in inner + outer
        for way, z in (("up", DEPTH), ("down", 1))
    }
    start(depth0.values())
    pass_on(0, ring_y)

    def row_copies(step, source, target):
        return [
            (
                way,
                pltpu.make_async_remote_copy(
                    src_ref=source.at[side],
                    dst_ref=target.at[side],
                    send_sem=y_send.at[step, side],
                    recv_sem=y_recv.at[step, side],
                    device_id=device,
                    device_id_type=MESH,
                ),
            )
            for side, way, device in ((0, "south", south), (1, "north", north))
        ]

    def pack_rows(source, target):
        for s in range(2):
            for z in range(DEPTH):
                target[0, s, z] = source[s, z + 1, BLOCK * groups - 1 : BLOCK * groups, :]
                target[1, s, z] = source[s, z + 1, 0:1, :]

    for k in outer:
        loads[k].wait()
    pack_rows(pad0, edge0)
    rows0 = row_copies(0, edge0, edge0_in)
    rows1 = row_copies(1, edge1, edge1_in)
    start(rows0)

    for copy in tables:
        copy.wait()
    load_classes.wait()

    def pick(bits, values):
        for bit in bits:
            values = [jnp.where(bit, high, low) for low, high in zip(values[::2], values[1::2])]
        return values[0]

    def look_up(target, values):
        splat = [[jnp.full((BLOCK, COLS), x, F32) for x in v] for v in values]

        def body(z, carry):
            for k in range(groups):
                c = cls[z, span(k), :]
                bits = [(c & bit) != 0 for bit in (1, 2, 4)]
                for s, v in enumerate(splat):
                    target[s, z, span(k), :] = pick(bits, v)
            return carry

        lax.fori_loop(0, DEPTH, body, 0)

    look_up(rates, [[diff_s[s, m] for m in range(NCLASS)] for s in range(2)])
    for k in inner:
        loads[k].wait()
    heard(0)
    pass_on(1, ring_y)

    sub = lax.broadcasted_iota(jnp.int32, (BLOCK, COLS), 0)
    col = lax.broadcasted_iota(jnp.int32, (BLOCK, COLS), 1)
    top, bottom = sub == 0, sub == BLOCK - 1
    left, right = col == 0, col == COLS - 1

    def around(source, edges, s, z, k):
        centre = source[s, z + 1, span(k), :]
        if k == 0:
            before = edges[0, s, z]
        else:
            before = source[s, z + 1, BLOCK * k - 1 : BLOCK * k, :]
        if k == groups - 1:
            after = edges[1, s, z]
        else:
            after = source[s, z + 1, BLOCK * k + BLOCK : BLOCK * k + BLOCK + 1, :]
        total = source[s, z + 2, span(k), :] + source[s, z, span(k), :]
        total = total + jnp.where(bottom, after, pltpu.roll(centre, BLOCK - 1, 0))
        total = total + jnp.where(top, before, pltpu.roll(centre, 1, 0))
        total = total + jnp.where(right, 0.0, pltpu.roll(centre, COLS - 1, 1))
        total = total + jnp.where(left, 0.0, pltpu.roll(centre, 1, 1))
        return centre, total - 6.0 * centre

    def advance(source, edges, z, k):
        u, lap_u = around(source, edges, 0, z, k)
        v, lap_v = around(source, edges, 1, z, k)
        growth = u * v * v
        new_u = u + rates[0, z, span(k), :] * lap_u - growth + FEED_RATE * (1.0 - u)
        new_v = v + rates[1, z, span(k), :] * lap_v + growth - (FEED_RATE + KILL_RATE) * v
        return new_u, new_v

    def first_update(z, k):
        new_u, new_v = advance(pad0, edge0_in, z, k)
        pad1[0, z + 1, span(k), :] = new_u
        pad1[1, z + 1, span(k), :] = new_v

    def clear_rows(target):
        def clear(way):
            for s in range(2):
                for z in range(DEPTH):
                    target[("south", "north").index(way), s, z] = jnp.zeros((1, COLS), F32)

        return clear

    def clear_depth(target, k):
        def clear(way):
            for s in range(2):
                target[s, 0 if way == "up" else DEPTH + 1, span(k), :] = jnp.zeros((BLOCK, COLS), F32)

        return clear

    def over_layers(update, blocks):
        def body(z, carry):
            for k in blocks:
                update(z, k)
            return carry

        if blocks:
            lax.fori_loop(1, DEPTH - 1, body, 0)

    over_layers(first_update, inner)
    heard(1)
    pass_on(2, ring_y)

    def outermost(k):
        for way, z, back in (("up", 0, "down"), ("down", DEPTH - 1, "up")):
            arrive([depth0[way, k]], clear_depth(pad0, k))
            first_update(z, k)
            start([depth1[back, k]])

    for k in inner:
        outermost(k)
    arrive(rows0, clear_rows(edge0_in))
    for k in outer:
        outermost(k)
    over_layers(first_update, outer)
    pack_rows(pad1, edge1)
    start(rows1)

    bins = [bin_s[m] for m in range(NCLASS)]
    scale = (1.0, 1.0, 1.0, -depth_step)
    look_up(look, [[trans_s[c, b] * scale[c] for b in bins] for c in range(4)])
    heard(2)
    pass_on(3, ring_x)

    def second_update(z, k):
        new_u, new_v = advance(pad1, edge1_in, z, k)
        final[0, z, span(k), :] = new_u
        final[1, z, span(k), :] = new_v
        passed = jnp.exp(look[3, z, span(k), :] * (0.25 + new_v * new_v))
        return new_u, passed

    for k in range(groups):
        mid[3, span(k), :] = jnp.ones((BLOCK, COLS), F32)
        for c in range(3):
            mid[c, span(k), :] = jnp.zeros((BLOCK, COLS), F32)

    def middle(z, k):
        new_u, passed = second_update(z, k)
        transmit = mid[3, span(k), :]
        weight = transmit * (1.0 - passed) * new_u
        for c in range(3):
            mid[c, span(k), :] = mid[c, span(k), :] + weight * look[c, z, span(k), :]
        mid[3, span(k), :] = transmit * passed

    over_layers(middle, inner)
    heard(3)
    pass_on(4, ring_x)
    arrive(rows1, clear_rows(edge1_in))
    over_layers(middle, outer)

    tiles = COLS // LANES // nc
    swaps = []
    for k in inner + outer:
        for way in ("up", "down"):
            arrive([depth1[way, k]], clear_depth(pad1, k))
        front_u, front_t = second_update(0, k)
        back_u, back_t = second_update(DEPTH - 1, k)
        front = (1.0 - front_t) * front_u
        transmit = mid[3, span(k), :]
        back = transmit * (1.0 - back_t) * back_u
        values = [
            front * look[c, 0, span(k), :] + front_t * (mid[c, span(k), :] + back * look[c, DEPTH - 1, span(k), :])
            for c in range(3)
        ]
        values.append(front_t * transmit * back_t)
        for half in range(nc):
            place = jnp.where(pc == half, pc, nc)
            for c in range(4):
                for t in range(tiles):
                    at = LANES * (tiles * half + t)
                    halves[place, k, pl.ds(4 * t + c, BLOCK, stride=8), :] = values[c][:, at : at + LANES]
        copy = pltpu.make_async_remote_copy(
            src_ref=halves.at[nc, k],
            dst_ref=halves.at[pc, k],
            send_sem=c_send.at[k],
            recv_sem=c_recv.at[k],
            device_id=mate,
            device_id_type=MESH,
        )
        copy.start()
        swaps.append((k, copy))

    place = lax.broadcasted_iota(jnp.int32, (8, LANES), 0)
    lower = place < 4
    is_light = (place == 3) | (place == 7)
    for k, copy in swaps:
        pltpu.make_async_remote_copy(
            src_ref=halves.at[nc, k],
            dst_ref=halves.at[1 - pc, k],
            send_sem=c_send.at[k],
            recv_sem=c_recv.at[k],
            device_id=mate,
            device_id_type=MESH,
        ).wait_recv()
        for row in range(BLOCK):
            near = halves[0, k, 8 * row : 8 * row + 8, :]
            light = jnp.where(
                lower, halves[0, k, 8 * row + 3 : 8 * row + 4, :], halves[0, k, 8 * row + 7 : 8 * row + 8, :]
            )
            merged[BLOCK * k + row] = jnp.where(is_light, 0.0, near) + light * halves[1, k, 8 * row : 8 * row + 8, :]

    heard(4)

    def hops(step):
        return min(step[0], ny - step[0]) + min(step[1], nx - step[1])

    steps = sorted([(dy, dx) for dy in range(ny) for dx in range(nx)][1:], key=hops, reverse=True)
    exchange = []
    for j, (dy, dx) in enumerate(steps):
        device = shifted(dy, dx)
        row = device[0] * nx + device[1]
        copy = pltpu.make_async_remote_copy(
            src_ref=merged.at[row],
            dst_ref=gathered.at[chip],
            send_sem=e_send.at[j],
            recv_sem=e_recv.at[chip],
            device_id=device,
            device_id_type=MESH,
        )
        copy.start()
        exchange.append(copy)
    gathered[chip] = merged[chip]
    for j, (dy, dx) in enumerate(steps):
        device = shifted(dy, dx)
        row = device[0] * nx + device[1]
        pltpu.make_async_remote_copy(
            src_ref=merged.at[row],
            dst_ref=gathered.at[row],
            send_sem=e_send.at[j],
            recv_sem=e_recv.at[row],
            device_id=device,
            device_id_type=MESH,
        ).wait_recv()
    total = transmit = None
    for i in range(ny * nx):
        light = jnp.where(lower, gathered[i, 3:4, :], gathered[i, 7:8, :])
        if i == 0:
            total, transmit = gathered[i], light
        else:
            total, transmit = total + transmit * gathered[i], transmit * light
    pixels[...] = jnp.where(is_light, 1.0 - transmit, total)

    for way, copy in list(depth0.values()) + list(depth1.values()) + rows0 + rows1:
        pl.when(sends[way])(copy.wait_send)
    for copy in [copy for _, copy in swaps] + exchange:
        copy.wait_send()


def place_outputs(final, pixels, species, image, sem):
    store = pltpu.make_async_copy(final, species, sem)
    store.start()
    image[:, 0:LANES] = pixels[0:4, :]
    image[:, LANES : 2 * LANES] = pixels[4:8, :]
    store.wait()


def build(mesh, sizes):
    ny, nx, nc, nz = sizes
    rows = ny * nx
    groups = rows // BLOCK
    block = (2, DEPTH, rows, COLS)
    padded = (2, DEPTH + 2, rows, COLS)
    edge = (2, 2, DEPTH, 1, COLS)
    vmem = pl.BlockSpec(memory_space=pltpu.VMEM)
    hbm = pl.BlockSpec(memory_space=pltpu.HBM)
    dma = pltpu.SemaphoreType.DMA

    def shards(fields, classes, diff_table, transfer, bin_table):
        depth_step = 2.0 / (DEPTH * ny * nx * nc)
        final, pixels = pl.pallas_call(
            functools.partial(kernel, sizes, depth_step),
            out_shape=(pltpu.VMEM(block, F32), pltpu.VMEM((8, LANES), F32)),
            in_specs=[hbm] * 5,
            out_specs=(vmem, vmem),
            scratch_shapes=[
                pltpu.VMEM(padded, F32),
                pltpu.VMEM(padded, F32),
                pltpu.VMEM((DEPTH, rows, COLS), jnp.int32),
                pltpu.VMEM(block, F32),
                pltpu.VMEM((4, DEPTH, rows, COLS), F32),
                pltpu.VMEM((4, rows, COLS), F32),
                pltpu.VMEM(edge, F32),
                pltpu.VMEM(edge, F32),
                pltpu.VMEM(edge, F32),
                pltpu.VMEM(edge, F32),
                pltpu.VMEM((nc + 1, groups, 8 * BLOCK, LANES), F32),
                pltpu.VMEM((rows, 8, LANES), F32),
                pltpu.VMEM((rows, 8, LANES), F32),
                pltpu.SMEM(diff_table.shape, F32),
                pltpu.SMEM(transfer.shape, F32),
                pltpu.SMEM(bin_table.shape, jnp.int32),
                dma((groups,)),
                dma((1,)),
                dma((3,)),
                dma((2, 2, groups)),
                dma((2, 2, groups)),
                dma((2, 2)),
                dma((2, 2)),
                dma((groups,)),
                dma((groups,)),
                dma((rows,)),
                dma((rows,)),
                pltpu.SemaphoreType.REGULAR((5, 2)),
            ],
            compiler_params=pltpu.CompilerParams(
                collective_id=0, has_side_effects=True, vmem_limit_bytes=20 * 2**20
            ),
            name="gray_scott",
        )(*(pltpu.with_memory_space_constraint(x, pltpu.HBM) for x in (fields, classes, diff_table, transfer, bin_table)))
        return pl.pallas_call(
            place_outputs,
            out_shape=(jax.ShapeDtypeStruct(block, F32), jax.ShapeDtypeStruct((4, 2 * LANES), F32)),
            in_specs=[vmem, vmem],
            out_specs=(hbm, vmem),
            scratch_shapes=[dma(())],
            compiler_params=pltpu.CompilerParams(vmem_limit_bytes=8 * 2**20),
            name="place_outputs",
        )(final, pixels)

    finer = Mesh(mesh.devices.reshape(sizes), NAMES)
    return jax.shard_map(
        shards,
        mesh=finer,
        in_specs=(P(None, GZ, "pz", None), P(GZ, "pz", None), P(), P(), P()),
        out_specs=(P(None, GZ, "pz", None), P(None, ("pz",) + GZ)),
        check_vma=False,
    )


def solution(mesh):
    return build(mesh, (8, 4, 2, mesh.shape["gy"]))
```

time: 104 us -> 29.6 us (0.28)
  the two profiles are of different devices: /device:TPU:192 before, /device:TPU:65 now
where the time goes in v2:
time: 29.6 us; the launch traced here: 29.5 us
  Pallas kernels  28.8 us (97%)
  between operations  0.64 us (2%)
    pallas_call x1, Pallas kernels, shards(): pl.pallas_call(functools.partial(kernel, sizes, depth_step), out_shape=(p...  27.2 us
    pallas_call x1, Pallas kernels, shards(): pl.pallas_call(place_outputs, out_shape=(jax.ShapeDtypeStruct(block, F32)...  1.57 us

profile of v2, /device:TPU:65, one launch (start us, length us, event | category | flops | bytes accessed | tf_op | source)
XLA Modules:
  0.0 29.5 jit_solution(17328487741824309618)
XLA Ops:
  0.6 27.2 %gray_scott.1 = (f32[2,8,32,512]{3,2,1,0:T(8,128)S(1)}, f32[8,128]{1,0:T(8,128)S(1)}) custom-call(f32[2,8,32,512]{3,2,1,0:T(8,128)} %fields.1, s32[8,32,512]{2,1,0:T(8,128)} %classes.1, f32[2,8]{1,0:T(2,128)} %diff_table.1, f32[4,16]{1,0:T(4,128)} %transfer.1, s32[8]{0:T(128)} %bin_table.1), custom_call_target="tpu_custom_call" | custom-call | tf_op jit(solution)/shard_map/gray_scott/pallas_call | solution.py:435
  27.9 1.6 %place_outputs.1 = (f32[2,8,32,512]{3,2,1,0:T(8,128)}, f32[4,256]{1,0:T(4,128)}) custom-call(f32[2,8,32,512]{3,2,1,0:T(8,128)S(1)} %get-tuple-element.4.final, f32[8,128]{1,0:T(8,128)S(1)} %get-tuple-element.5.pixels), custom_call_target="tpu_custom_call" | custom-call | tf_op jit(solution)/shard_map/place_outputs/pallas_call | solution.py:475

commit v3 on v2

--- a/solution.py
+++ b/solution.py
@@ -15,6 +15,7 @@
 KILL_RATE = 0.06
 NCLASS = 8
 DEPTH = 8
+UNROLL = 3
 COLS = 512
 LANES = 128
 BLOCK = 8
@@ -77,6 +78,21 @@
     load_classes = pltpu.make_async_copy(classes, cls, class_sem.at[0])
     load_classes.start()
 
+    def clear_depth(layer):
+        for pad in (pad0, pad1):
+            for s in range(2):
+                pad[s, layer] = jnp.zeros(pad.shape[2:], F32)
+
+    def clear_rows(side):
+        for edge in (edge0_in, edge1_in):
+            for s in range(2):
+                edge[side, s] = jnp.zeros(edge.shape[2:], F32)
+
+    pl.when(jnp.logical_not(has_below))(functools.partial(clear_depth, 0))
+    pl.when(jnp.logical_not(has_above))(functools.partial(clear_depth, DEPTH + 1))
+    pl.when(jnp.logical_not(has_north))(functools.partial(clear_rows, 0))
+    pl.when(jnp.logical_not(has_south))(functools.partial(clear_rows, 1))
+
     barrier = pltpu.get_barrier_semaphore()
 
     def greet(device):
@@ -109,10 +125,9 @@
         for way, copy in copies:
             pl.when(sends[way])(copy.start)
 
-    def arrive(copies, clear):
+    def arrive(copies):
         for way, copy in copies:
             pl.when(arrives[way])(copy.wait_recv)
-            pl.when(jnp.logical_not(arrives[way]))(functools.partial(clear, way))
 
     def depth_copy(step, way, k, source, target):
         side = ("up", "down").index(way)
@@ -238,43 +253,31 @@
         pad1[0, z + 1, span(k), :] = new_u
         pad1[1, z + 1, span(k), :] = new_v
 
-    def clear_rows(target):
-        def clear(way):
-            for s in range(2):
-                for z in range(DEPTH):
-                    target[("south", "north").index(way), s, z] = jnp.zeros((1, COLS), F32)
-
-        return clear
-
-    def clear_depth(target, k):
-        def clear(way):
-            for s in range(2):
-                target[s, 0 if way == "up" else DEPTH + 1, span(k), :] = jnp.zeros((BLOCK, COLS), F32)
-
-        return clear
-
     def over_layers(update, blocks):
-        def body(z, carry):
-            for k in blocks:
-                update(z, k)
+        def body(i, carry):
+            for j in range(UNROLL):
+                for k in blocks:
+                    update(1 + UNROLL * i + j, k)
             return carry
 
         if blocks:
-            lax.fori_loop(1, DEPTH - 1, body, 0)
+            lax.fori_loop(0, (DEPTH - 2) // UNROLL, body, 0)
 
     over_layers(first_update, inner)
     heard(1)
     pass_on(2, ring_y)
 
     def outermost(k):
-        for way, z, back in (("up", 0, "down"), ("down", DEPTH - 1, "up")):
-            arrive([depth0[way, k]], clear_depth(pad0, k))
+        for way in ("up", "down"):
+            arrive([depth0[way, k]])
+        for z in (0, DEPTH - 1):
             first_update(z, k)
-            start([depth1[back, k]])
+        for way in ("down", "up"):
+            start([depth1[way, k]])
 
     for k in inner:
         outermost(k)
-    arrive(rows0, clear_rows(edge0_in))
+    arrive(rows0)
     for k in outer:
         outermost(k)
     over_layers(first_update, outer)
@@ -310,14 +313,14 @@
     over_layers(middle, inner)
     heard(3)
     pass_on(4, ring_x)
-    arrive(rows1, clear_rows(edge1_in))
+    arrive(rows1)
     over_layers(middle, outer)
 
     tiles = COLS // LANES // nc
     swaps = []
     for k in inner + outer:
         for way in ("up", "down"):
-            arrive([depth1[way, k]], clear_depth(pad1, k))
+            arrive([depth1[way, k]])
         front_u, front_t = second_update(0, k)
         back_u, back_t = second_update(DEPTH - 1, k)
         front = (1.0 - front_t) * front_u
@@ -396,13 +399,17 @@
             device_id=device,
             device_id_type=MESH,
         ).wait_recv()
-    total = transmit = None
-    for i in range(ny * nx):
-        light = jnp.where(lower, gathered[i, 3:4, :], gathered[i, 7:8, :])
-        if i == 0:
-            total, transmit = gathered[i], light
-        else:
+    runs = []
+    for first in range(0, ny * nx, 4):
+        total = gathered[first]
+        transmit = jnp.where(lower, gathered[first, 3:4, :], gathered[first, 7:8, :])
+        for i in range(first + 1, first + 4):
+            light = jnp.where(lower, gathered[i, 3:4, :], gathered[i, 7:8, :])
             total, transmit = total + transmit * gathered[i], transmit * light
+        runs.append((total, transmit))
+    while len(runs) > 1:
+        runs = [(a + s * b, s * t) for (a, s), (b, t) in zip(runs[::2], runs[1::2])]
+    total, transmit = runs[0]
     pixels[...] = jnp.where(is_light, 1.0 - transmit, total)
 
     for way, copy in list(depth0.values()) + list(depth1.values()) + rows0 + rows1:
@@ -411,12 +418,15 @@
         copy.wait_send()
 
 
-def place_outputs(final, pixels, species, image, sem):
-    store = pltpu.make_async_copy(final, species, sem)
+def place_outputs(final, pixels, species, image, picture, sems):
+    store = pltpu.make_async_copy(final, species, sems.at[0])
     store.start()
-    image[:, 0:LANES] = pixels[0:4, :]
-    image[:, LANES : 2 * LANES] = pixels[4:8, :]
+    picture[:, 0:LANES] = pixels[0:4, :]
+    picture[:, LANES : 2 * LANES] = pixels[4:8, :]
+    show = pltpu.make_async_copy(picture, image, sems.at[1])
+    show.start()
     store.wait()
+    show.wait()
 
 
 def build(mesh, sizes):
@@ -476,8 +486,8 @@
             place_outputs,
             out_shape=(jax.ShapeDtypeStruct(block, F32), jax.ShapeDtypeStruct((4, 2 * LANES), F32)),
             in_specs=[vmem, vmem],
-            out_specs=(hbm, vmem),
-            scratch_shapes=[dma(())],
+            out_specs=(hbm, hbm),
+            scratch_shapes=[pltpu.VMEM((4, 2 * LANES), F32), dma((2,))],
             compiler_params=pltpu.CompilerParams(vmem_limit_bytes=8 * 2**20),
             name="place_outputs",
         )(final, pixels)

time: 29.6 us -> 28.3 us (0.956)
  Pallas kernels: 28.8 us -> 27.5 us
    pallas_call x1, Pallas kernels: 27.2 us -> 26.5 us  [shards(): pl.pallas_call(functools.partial(kernel, sizes, depth_step), out_shape=(p...]
    pallas_call x1, Pallas kernels: 1.57 us -> 0.99 us  [shards(): pl.pallas_call(place_outputs, out_shape=(jax.ShapeDtypeStruct(block, F32)...]
where the time goes in v3:
time: 28.3 us; the launch traced here: 28.1 us
  Pallas kernels  27.5 us (97%)
  between operations  0.64 us (2%)
    pallas_call x1, Pallas kernels, shards(): pl.pallas_call(functools.partial(kernel, sizes, depth_step), out_shape=(p...  26.5 us
    pallas_call x1, Pallas kernels, shards(): pl.pallas_call(place_outputs, out_shape=(jax.ShapeDtypeStruct(block, F32)...  0.99 us

profile of v3, /device:TPU:65, one launch (start us, length us, event | category | flops | bytes accessed | tf_op | source)
XLA Modules:
  0.0 28.1 jit_solution(15280465207281136029)
XLA Ops:
  0.6 26.5 %gray_scott.1 = (f32[2,8,32,512]{3,2,1,0:T(8,128)S(1)}, f32[8,128]{1,0:T(8,128)S(1)}) custom-call(f32[2,8,32,512]{3,2,1,0:T(8,128)} %fields.1, s32[8,32,512]{2,1,0:T(8,128)} %classes.1, f32[2,8]{1,0:T(2,128)} %diff_table.1, f32[4,16]{1,0:T(4,128)} %transfer.1, s32[8]{0:T(128)} %bin_table.1), custom_call_target="tpu_custom_call" | custom-call | tf_op jit(solution)/shard_map/gray_scott/pallas_call | solution.py:445
  27.1 1.0 %place_outputs.1 = (f32[2,8,32,512]{3,2,1,0:T(8,128)}, f32[4,256]{1,0:T(4,128)}) custom-call(f32[2,8,32,512]{3,2,1,0:T(8,128)S(1)} %get-tuple-element.4.final, f32[8,128]{1,0:T(8,128)S(1)} %get-tuple-element.5.pixels), custom_call_target="tpu_custom_call" | custom-call | tf_op jit(solution)/shard_map/place_outputs/pallas_call | solution.py:485

commit v4 on v3

--- a/solution.py
+++ b/solution.py
@@ -59,6 +59,21 @@
     def shifted(dy, dx):
         return (lax.rem(py + dy, ny), lax.rem(px + dx, nx), pc, pz)
 
+    barrier = pltpu.get_barrier_semaphore()
+
+    def greet(device):
+        pl.semaphore_signal(barrier, inc=1, device_id=device, device_id_type=MESH)
+
+    ring_y = (shifted(1, 0), shifted(ny - 1, 0))
+    ring_x = (shifted(0, 1), shifted(0, nx - 1))
+    partners = (mate,) + ring_x + ring_y
+    others = ((has_above, above), (has_below, below), (has_north, north), (has_south, south))
+    count = len(partners)
+    for exists, device in others:
+        pl.when(exists)(functools.partial(greet, device))
+        count = count + jnp.where(exists, 1, 0)
+    for device in partners:
+        greet(device)
     loads = {
         k: pltpu.make_async_copy(
             fields.at[:, :, pl.ds(BLOCK * k, BLOCK)],
@@ -78,36 +93,6 @@
     load_classes = pltpu.make_async_copy(classes, cls, class_sem.at[0])
     load_classes.start()
 
-    def clear_depth(layer):
-        for pad in (pad0, pad1):
-            for s in range(2):
-                pad[s, layer] = jnp.zeros(pad.shape[2:], F32)
-
-    def clear_rows(side):
-        for edge in (edge0_in, edge1_in):
-            for s in range(2):
-                edge[side, s] = jnp.zeros(edge.shape[2:], F32)
-
-    pl.when(jnp.logical_not(has_below))(functools.partial(clear_depth, 0))
-    pl.when(jnp.logical_not(has_above))(functools.partial(clear_depth, DEPTH + 1))
-    pl.when(jnp.logical_not(has_north))(functools.partial(clear_rows, 0))
-    pl.when(jnp.logical_not(has_south))(functools.partial(clear_rows, 1))
-
-    barrier = pltpu.get_barrier_semaphore()
-
-    def greet(device):
-        pl.semaphore_signal(barrier, inc=1, device_id=device, device_id_type=MESH)
-
-    ring_y = (shifted(1, 0), shifted(ny - 1, 0))
-    ring_x = (shifted(0, 1), shifted(0, nx - 1))
-    partners = (mate,) + ring_x + ring_y
-    others = ((has_above, above), (has_below, below), (has_north, north), (has_south, south))
-    count = len(partners)
-    for exists, device in others:
-        pl.when(exists)(functools.partial(greet, device))
-        count = count + jnp.where(exists, 1, 0)
-    for device in partners:
-        greet(device)
     pl.semaphore_wait(barrier, count)
 
     def pass_on(r, ring):
@@ -189,6 +174,22 @@
     rows0 = row_copies(0, edge0, edge0_in)
     rows1 = row_copies(1, edge1, edge1_in)
     start(rows0)
+
+    def clear_depth(layer):
+        for pad in (pad0, pad1):
+            for s in range(2):
+                pad[s, layer] = jnp.zeros(pad.shape[2:], F32)
+
+    def clear_rows(side):
+        for edge in (edge0_in, edge1_in):
+            for s in range(2):
+                edge[side, s] = jnp.zeros(edge.shape[2:], F32)
+
+    pl.when(jnp.logical_not(has_below))(functools.partial(clear_depth, 0))
+    pl.when(jnp.logical_not(has_above))(functools.partial(clear_depth, DEPTH + 1))
+    pl.when(jnp.logical_not(has_north))(functools.partial(clear_rows, 0))
+    pl.when(jnp.logical_not(has_south))(functools.partial(clear_rows, 1))
+
 
     for copy in tables:
         copy.wait()
@@ -373,32 +374,33 @@
         return min(step[0], ny - step[0]) + min(step[1], nx - step[1])
 
     steps = sorted([(dy, dx) for dy in range(ny) for dx in range(nx)][1:], key=hops, reverse=True)
-    exchange = []
-    for j, (dy, dx) in enumerate(steps):
-        device = shifted(dy, dx)
-        row = device[0] * nx + device[1]
-        copy = pltpu.make_async_remote_copy(
-            src_ref=merged.at[row],
-            dst_ref=gathered.at[chip],
-            send_sem=e_send.at[j],
-            recv_sem=e_recv.at[chip],
-            device_id=device,
-            device_id_type=MESH,
-        )
-        copy.start()
-        exchange.append(copy)
-    gathered[chip] = merged[chip]
-    for j, (dy, dx) in enumerate(steps):
+    for dy, dx in steps:
         device = shifted(dy, dx)
         row = device[0] * nx + device[1]
         pltpu.make_async_remote_copy(
             src_ref=merged.at[row],
-            dst_ref=gathered.at[row],
-            send_sem=e_send.at[j],
-            recv_sem=e_recv.at[row],
+            dst_ref=gathered.at[chip],
+            send_sem=e_send.at[0],
+            recv_sem=e_recv.at[0],
             device_id=device,
             device_id_type=MESH,
-        ).wait_recv()
+        ).start()
+    gathered[chip] = merged[chip]
+    for way, copy in list(depth0.values()) + list(depth1.values()) + rows0 + rows1:
+        pl.when(sends[way])(copy.wait_send)
+    for _, copy in swaps:
+        copy.wait_send()
+    others = pl.ds(0, ny * nx - 1)
+    everything = pltpu.make_async_remote_copy(
+        src_ref=merged.at[others],
+        dst_ref=gathered.at[others],
+        send_sem=e_send.at[0],
+        recv_sem=e_recv.at[0],
+        device_id=mate,
+        device_id_type=MESH,
+    )
+    everything.wait_send()
+    everything.wait_recv()
     runs = []
     for first in range(0, ny * nx, 4):
         total = gathered[first]
@@ -411,11 +413,6 @@
         runs = [(a + s * b, s * t) for (a, s), (b, t) in zip(runs[::2], runs[1::2])]
     total, transmit = runs[0]
     pixels[...] = jnp.where(is_light, 1.0 - transmit, total)
-
-    for way, copy in list(depth0.values()) + list(depth1.values()) + rows0 + rows1:
-        pl.when(sends[way])(copy.wait_send)
-    for copy in [copy for _, copy in swaps] + exchange:
-        copy.wait_send()
 
 
 def place_outputs(final, pixels, species, image, picture, sems):
@@ -473,8 +470,8 @@
                 dma((2, 2)),
                 dma((groups,)),
                 dma((groups,)),
-                dma((rows,)),
-                dma((rows,)),
+                dma((1,)),
+                dma((1,)),
                 pltpu.SemaphoreType.REGULAR((5, 2)),
             ],
             compiler_params=pltpu.CompilerParams(

time: 28.3 us -> 27.7 us (0.979)
  Pallas kernels: 27.5 us -> 26.9 us
    pallas_call x1, Pallas kernels: 26.5 us -> 25.9 us  [shards(): pl.pallas_call(functools.partial(kernel, sizes, depth_step), out_shape=(p...]
where the time goes in v4:
time: 27.7 us; the launch traced here: 27.5 us
  Pallas kernels  26.9 us (97%)
  between operations  0.64 us (2%)
    pallas_call x1, Pallas kernels, shards(): pl.pallas_call(functools.partial(kernel, sizes, depth_step), out_shape=(p...  25.9 us
    pallas_call x1, Pallas kernels, shards(): pl.pallas_call(place_outputs, out_shape=(jax.ShapeDtypeStruct(block, F32)...  0.99 us

profile of v4, /device:TPU:65, one launch (start us, length us, event | category | flops | bytes accessed | tf_op | source)
XLA Modules:
  0.0 27.5 jit_solution(17274411876864245276)
XLA Ops:
  0.6 25.9 %gray_scott.1 = (f32[2,8,32,512]{3,2,1,0:T(8,128)S(1)}, f32[8,128]{1,0:T(8,128)S(1)}) custom-call(f32[2,8,32,512]{3,2,1,0:T(8,128)} %fields.1, s32[8,32,512]{2,1,0:T(8,128)} %classes.1, f32[2,8]{1,0:T(2,128)} %diff_table.1, f32[4,16]{1,0:T(4,128)} %transfer.1, s32[8]{0:T(128)} %bin_table.1), custom_call_target="tpu_custom_call" | custom-call | tf_op jit(solution)/shard_map/gray_scott/pallas_call | solution.py:442
  26.5 1.0 %place_outputs.1 = (f32[2,8,32,512]{3,2,1,0:T(8,128)}, f32[4,256]{1,0:T(4,128)}) custom-call(f32[2,8,32,512]{3,2,1,0:T(8,128)S(1)} %get-tuple-element.4.final, f32[8,128]{1,0:T(8,128)S(1)} %get-tuple-element.5.pixels), custom_call_target="tpu_custom_call" | custom-call | tf_op jit(solution)/shard_map/place_outputs/pallas_call | solution.py:482

commit v5 on v4

--- a/solution.py
+++ b/solution.py
@@ -220,9 +220,9 @@
     pass_on(1, ring_y)
 
     sub = lax.broadcasted_iota(jnp.int32, (BLOCK, COLS), 0)
-    col = lax.broadcasted_iota(jnp.int32, (BLOCK, COLS), 1)
     top, bottom = sub == 0, sub == BLOCK - 1
-    left, right = col == 0, col == COLS - 1
+    lane = lax.broadcasted_iota(jnp.int32, (BLOCK, LANES), 1)
+    left, right = lane == 0, lane == LANES - 1
 
     def around(source, edges, s, z, k):
         centre = source[s, z + 1, span(k), :]
@@ -237,16 +237,20 @@
         total = source[s, z + 2, span(k), :] + source[s, z, span(k), :]
         total = total + jnp.where(bottom, after, pltpu.roll(centre, BLOCK - 1, 0))
         total = total + jnp.where(top, before, pltpu.roll(centre, 1, 0))
-        total = total + jnp.where(right, 0.0, pltpu.roll(centre, COLS - 1, 1))
-        total = total + jnp.where(left, 0.0, pltpu.roll(centre, 1, 1))
+        cut = [centre[:, LANES * t : LANES * t + LANES] for t in range(COLS // LANES)]
+        zero = jnp.zeros((BLOCK, LANES), F32)
+        after_cut, before_cut = cut[1:] + [zero], [zero] + cut[:-1]
+        right_side = [pltpu.roll(jnp.where(left, b, a), LANES - 1, 1) for a, b in zip(cut, after_cut)]
+        left_side = [pltpu.roll(jnp.where(right, b, a), 1, 1) for a, b in zip(cut, before_cut)]
+        total = total + (jnp.concatenate(right_side, 1) + jnp.concatenate(left_side, 1))
         return centre, total - 6.0 * centre
 
     def advance(source, edges, z, k):
         u, lap_u = around(source, edges, 0, z, k)
         v, lap_v = around(source, edges, 1, z, k)
         growth = u * v * v
-        new_u = u + rates[0, z, span(k), :] * lap_u - growth + FEED_RATE * (1.0 - u)
-        new_v = v + rates[1, z, span(k), :] * lap_v + growth - (FEED_RATE + KILL_RATE) * v
+        new_u = (1.0 - FEED_RATE) * u + rates[0, z, span(k), :] * lap_u + (FEED_RATE - growth)
+        new_v = (1.0 - FEED_RATE - KILL_RATE) * v + rates[1, z, span(k), :] * lap_v + growth
         return new_u, new_v
 
     def first_update(z, k):
@@ -306,10 +310,11 @@
     def middle(z, k):
         new_u, passed = second_update(z, k)
         transmit = mid[3, span(k), :]
-        weight = transmit * (1.0 - passed) * new_u
+        left_over = transmit * passed
+        weight = (transmit - left_over) * new_u
         for c in range(3):
             mid[c, span(k), :] = mid[c, span(k), :] + weight * look[c, z, span(k), :]
-        mid[3, span(k), :] = transmit * passed
+        mid[3, span(k), :] = left_over
 
     over_layers(middle, inner)
     heard(3)

time: 27.7 us -> 27.6 us (level)
  no operation moved by 1% of the time
where the time goes in v5:
time: 27.6 us; the launch traced here: 27.4 us
  Pallas kernels  26.8 us (97%)
  between operations  0.64 us (2%)
    pallas_call x1, Pallas kernels, shards(): pl.pallas_call(functools.partial(kernel, sizes, depth_step), out_shape=(p...  25.8 us
    pallas_call x1, Pallas kernels, shards(): pl.pallas_call(place_outputs, out_shape=(jax.ShapeDtypeStruct(block, F32)...  0.99 us

profile of v5, /device:TPU:65, one launch (start us, length us, event | category | flops | bytes accessed | tf_op | source)
XLA Modules:
  0.0 27.4 jit_solution(6986374905448269205)
XLA Ops:
  0.6 25.8 %gray_scott.1 = (f32[2,8,32,512]{3,2,1,0:T(8,128)S(1)}, f32[8,128]{1,0:T(8,128)S(1)}) custom-call(f32[2,8,32,512]{3,2,1,0:T(8,128)} %fields.1, s32[8,32,512]{2,1,0:T(8,128)} %classes.1, f32[2,8]{1,0:T(2,128)} %diff_table.1, f32[4,16]{1,0:T(4,128)} %transfer.1, s32[8]{0:T(128)} %bin_table.1), custom_call_target="tpu_custom_call" | custom-call | tf_op jit(solution)/shard_map/gray_scott/pallas_call | solution.py:447
  26.4 1.0 %place_outputs.1 = (f32[2,8,32,512]{3,2,1,0:T(8,128)}, f32[4,256]{1,0:T(4,128)}) custom-call(f32[2,8,32,512]{3,2,1,0:T(8,128)S(1)} %get-tuple-element.4.final, f32[8,128]{1,0:T(8,128)S(1)} %get-tuple-element.5.pixels), custom_call_target="tpu_custom_call" | custom-call | tf_op jit(solution)/shard_map/place_outputs/pallas_call | solution.py:487
